TPU v7x, 128 devices: a whole 4x4x4 slice. The times are simulated.
128 devices in a mesh: lon: 32 (over x, y, z_lo), lat: 4 (over z_hi, core).
Axes of the slice: x: 4, y: 4, z: 4 (z_hi: 2, z_lo: 2; z = z_hi * 2 + z_lo), core: 2. Of those that a mesh axis runs over, the one named last changes fastest.
Arguments:
- adjoint_in: float32 [72, 2, 256, 4096], P(None, None, 'lat', 'lon'), may hold values from -6 to 6
- courant: float32 [2, 72, 256, 4096], P(None, None, 'lat', 'lon'), may hold values from -0.5 to 0.5
- mixing: float32 [71, 256, 4096], P(None, 'lat', 'lon'), may hold values from 0.05 to 4
- kernel_blocks: float32 [72, 262144], P(None, ('lon', 'lat')), may hold values from -6 to 6
- sounding_dest: int32 [262144, 1], P(('lon', 'lat')), may hold values from 0 to 127; in each aligned block of 2048 rows (0 to 2047, 2048 to 4095, ...) at most 64 rows name the same one
- sounding_cell: int32 [262144], P(('lon', 'lat')), may hold values from 0 to 16383
Outputs:
- adjoint_out: float32 [72, 2, 256, 4096], P(None, None, 'lat', 'lon')
- flux_grad: float32 [2, 256, 4096], P(None, 'lat', 'lon')
Inputs may be any that keep to these rules, and one draw needn't show every extreme that they name: `sounding_dest`: in each device's block of 2048 soundings at most 64 name one owner device, and some owner gets exactly 64 of them.
All inputs are finite; a program needn't handle non-finite values.
Results may differ from a plain program's by a relative error of at most 0.00002.
Values sent between devices are 32-bit elements; how exact they have to be, the bound alone decides.
A program may use at most 192 MiB of HBM per device.

v0:
```python
import functools
import jax
import jax.numpy as jnp
from jax import lax
from jax.experimental import pallas as pl
from jax.experimental.pallas import tpu as pltpu
from jax.sharding import PartitionSpec as P

MESH = pl.DeviceIdType.MESH
ANY = pl.BlockSpec(memory_space=pl.ANY)
LANES = 128
HALF = 40
STREAMS = 4
VMEM_LIMIT = 60 * 1024 * 1024


def lane_iota(shape):
    return lax.broadcasted_iota(jnp.int32, shape, len(shape) - 1)


def pack_kernel(
    devices, capacity, levels, blocks_ref, dest_ref, cell_ref, out_ref, rows, slots, order, order_smem, sem
):
    held = blocks_ref.shape[1]
    chunks = held // LANES
    row_id = lax.broadcasted_iota(jnp.int32, (LANES, LANES), 0)
    col_id = lax.broadcasted_iota(jnp.int32, (LANES, LANES), 1)
    before = jnp.where(row_id < col_id, 1.0, 0.0).astype(jnp.bfloat16)
    ones = jnp.ones((LANES, LANES), jnp.bfloat16)
    base = jnp.zeros((LANES, LANES), jnp.float32)
    for chunk in range(chunks):
        owner = dest_ref[chunk : chunk + 1, :]
        hot = jnp.broadcast_to(owner, (LANES, LANES)) == row_id
        hot_f = jnp.where(hot, 1.0, 0.0)
        hot_b = hot_f.astype(jnp.bfloat16)
        earlier = jnp.dot(hot_b, before, preferred_element_type=jnp.float32)
        rank = jnp.sum(hot_f * (earlier + base), axis=0, keepdims=True)
        order[chunk : chunk + 1, :] = owner * capacity + rank.astype(jnp.int32)
        base = base + jnp.dot(hot_b, ones, preferred_element_type=jnp.float32)
    to_smem = pltpu.make_async_copy(order, order_smem, sem)
    to_smem.start()
    blank = jnp.where(lane_iota((64, LANES)) == levels, -1.0, 0.0)

    @pl.loop(0, devices * capacity // 64)
    def _(i):
        slots[pl.ds(pl.multiple_of(i * 64, 64), 64), :] = blank

    for chunk in range(chunks):
        span = slice(chunk * LANES, (chunk + 1) * LANES)
        tall = jnp.concatenate(
            [
                blocks_ref[:, span],
                jnp.broadcast_to(cell_ref[chunk : chunk + 1, :].astype(jnp.float32), (8, LANES)),
                jnp.zeros((LANES - levels - 8, LANES), jnp.float32),
            ],
            axis=0,
        )
        rows[span, :] = tall.T
    to_smem.wait()

    @pl.loop(0, chunks)
    def _(chunk):
        @pl.loop(0, LANES // 16)
        def _(part):
            for i in range(16):
                at = part * 16 + i
                slots[pl.ds(order_smem[chunk, at], 1), :] = rows[pl.ds(chunk * LANES + at, 1), :]

    low = lane_iota((HALF, LANES)) < capacity

    @pl.loop(0, devices // 2)
    def _(pair):
        wide = slots[pl.ds(pl.multiple_of(pair * LANES, LANES), LANES), :].T
        first, second = wide[:HALF], wide[HALF : 2 * HALF]
        out_ref[2 * pair] = jnp.where(low, first, pltpu.roll(second, capacity, 1))
        out_ref[2 * pair + 1] = jnp.where(low, pltpu.roll(first, capacity, 1), second)


def pack(kernel_blocks, owner, cell, devices, capacity):
    levels, held = kernel_blocks.shape
    return pl.pallas_call(
        functools.partial(pack_kernel, devices, capacity, levels),
        out_shape=jax.ShapeDtypeStruct((devices, HALF, LANES), jnp.float32),
        in_specs=[pl.BlockSpec(memory_space=pltpu.VMEM)] * 3,
        out_specs=pl.BlockSpec(memory_space=pltpu.VMEM),
        scratch_shapes=[
            pltpu.VMEM((held, LANES), jnp.float32),
            pltpu.VMEM((devices * capacity, LANES), jnp.float32),
            pltpu.VMEM((held // LANES, LANES), jnp.int32),
            pltpu.SMEM((held // LANES, LANES), jnp.int32),
            pltpu.SemaphoreType.DMA,
        ],
        compiler_params=pltpu.CompilerParams(vmem_limit_bytes=VMEM_LIMIT),
        name="pack_soundings",
    )(kernel_blocks, owner, cell)


def transport_body(
    lon_count,
    lat_count,
    after_entry,
    before_exit,
    a_hbm,
    c_hbm,
    m_hbm,
    out_hbm,
    a_ref,
    c_ref,
    m_ref,
    vbuf,
    rbuf,
    obuf,
    send_n,
    send_s,
    send_e,
    send_w,
    from_s,
    from_n,
    from_w,
    from_e,
    merged,
    load_sem,
    store_sem,
    send_sem,
    recv_sem,
):
    levels, tracers, band, tile = a_ref.shape
    lon, lat = lax.axis_index("lon"), lax.axis_index("lat")
    north = {"lon": lon, "lat": lax.rem(lat + 1, lat_count)}
    south = {"lon": lon, "lat": lax.rem(lat + lat_count - 1, lat_count)}
    east = {"lon": lax.rem(lon + 1, lon_count), "lat": lat}
    west = {"lon": lax.rem(lon + lon_count - 1, lon_count), "lat": lat}

    loads = [
        pltpu.make_async_copy(m_hbm, m_ref, load_sem.at[0]),
        pltpu.make_async_copy(a_hbm, a_ref, load_sem.at[1]),
        pltpu.make_async_copy(c_hbm, c_ref, load_sem.at[2]),
    ]
    for load in loads:
        load.start()
    after_entry()
    loads[0].wait()
    loads[1].wait()

    mix = m_ref[0]
    inverse = 1.0 / (1.0 + mix)
    ratio = mix * inverse
    solved = a_ref[0] * inverse[None]
    rbuf[0] = ratio
    vbuf[0] = solved

    def down(k, carry):
        mix_above, ratio, solved = carry
        mix = m_ref[k]
        inverse = 1.0 / (1.0 + mix_above + mix - mix_above * ratio)
        ratio = mix * inverse
        solved = (a_ref[k] + mix_above[None] * solved) * inverse[None]
        rbuf[k] = ratio
        vbuf[k] = solved
        return mix, ratio, solved

    mix, ratio, solved = lax.fori_loop(1, levels - 1, down, (mix, ratio, solved))
    inverse = 1.0 / (1.0 + mix - mix * ratio)
    solved = (a_ref[levels - 1] + mix[None] * solved) * inverse[None]

    def keep(k, solved):
        vbuf[k] = solved
        for t in range(tracers):
            send_s[pl.ds(tracers * k + t, 1), :] = solved[t, 0:1, :]
            send_n[pl.ds(tracers * k + t, 1), :] = solved[t, band - 1 : band, :]

    keep(levels - 1, solved)

    def up(i, solved):
        k = levels - 2 - i
        solved = vbuf[k] + rbuf[k][None] * solved
        keep(k, solved)
        return solved

    lax.fori_loop(0, levels - 1, up, solved)

    loads[2].wait()
    row = lax.broadcasted_iota(jnp.int32, (band, tile), 0)
    lane = lane_iota((band, tile))
    top = row == band - 1
    edge = jnp.where(lat == lat_count - 1, 0.0, 1.0)

    @pl.loop(0, levels)
    def _(k):
        send_n[pl.ds(levels * tracers + k, 1), :] = c_ref[1, k, band - 1 : band, :] * edge

    def remote(index, src, dst, to):
        return pltpu.make_async_remote_copy(
            src_ref=src, dst_ref=dst, send_sem=send_sem.at[index], recv_sem=recv_sem.at[index],
            device_id=to, device_id_type=MESH,
        )

    to_north = remote(0, send_n, from_s, north)
    to_south = remote(1, send_s, from_n, south)
    to_north.start()
    to_south.start()
    to_north.wait()
    to_south.wait()

    keep_top = jnp.where(top, edge, 1.0)
    zero = jnp.zeros((band, tile), jnp.float32)
    for t in range(tracers):

        def sweep(k, carry):
            first, last, wind_last = carry
            face = c_ref[1, k] * keep_top
            cells = vbuf[k, t]
            above = from_n[pl.ds(tracers * k + t, 1), :]
            below = from_s[pl.ds(tracers * k + t, 1), :]
            face_below = from_s[pl.ds(levels * tracers + k, 1), :]
            rise = jnp.where(top, above, pltpu.roll(cells, band - 1, 0)) - cells
            incoming = jnp.minimum(face, 0.0) * rise
            incoming = jnp.where(
                row == 0,
                jnp.minimum(face_below, 0.0) * (cells - below),
                pltpu.roll(incoming, 1, 0),
            )
            cells = cells + jnp.maximum(face, 0.0) * rise + incoming
            vbuf[k, t] = cells
            turned = pltpu.roll(cells, k, 1)
            at_first = lane == k
            at_last = lane == lax.rem(k + tile - 1, tile)
            first = jnp.where(at_first, turned, first)
            last = jnp.where(at_last, turned, last)
            if t == 0:
                wind_last = jnp.where(at_last, pltpu.roll(c_ref[0, k], k, 1), wind_last)
            return first, last, wind_last

        first, last, wind_last = lax.fori_loop(0, levels, sweep, (zero, zero, zero))
        send_w[t] = first
        send_e[t] = last
        if t == 0:
            send_e[tracers] = wind_last

    to_east = remote(2, send_e, from_w, east)
    to_west = remote(3, send_w, from_e, west)
    to_east.start()
    to_west.start()
    to_east.wait()
    to_west.wait()
    even = lax.rem(lane, 2) == 0
    for t in range(tracers):
        eastern, western = from_e[t], pltpu.roll(from_w[t], 2, 1)
        merged[t, 0] = jnp.where(even, eastern, western)
        merged[t, 1] = jnp.where(even, western, eastern)

    group = 8

    def stored(j):
        span = pl.ds(j * group, group)
        return pltpu.make_async_copy(obuf.at[span], out_hbm.at[span], store_sem.at[j])

    @pl.loop(0, levels // group)
    def _(j):
        @pl.loop(0, group // 2)
        def _(i):
            for parity in range(2):
                k = j * group + 2 * i + parity
                face = c_ref[0, k]
                face_west = pltpu.roll(from_w[tracers], lax.rem(tile + 1 - k, tile), 1)
                for t in range(tracers):
                    cells = vbuf[k, t]
                    sides = pltpu.roll(merged[t, parity], tile - 1 - k, 1)
                    rise = jnp.where(lane == tile - 1, sides, pltpu.roll(cells, tile - 1, 1)) - cells
                    incoming = jnp.minimum(face, 0.0) * rise
                    incoming = jnp.where(
                        lane == 0,
                        jnp.minimum(face_west, 0.0) * (cells - sides),
                        pltpu.roll(incoming, 1, 1),
                    )
                    obuf[k, t] = cells + jnp.maximum(face, 0.0) * rise + incoming

        stored(j).start()

    before_exit()

    @pl.loop(0, levels // group)
    def _(j):
        stored(j).wait()


def step_scratch(levels, tracers, band, tile):
    f32 = jnp.float32
    return [
        pltpu.VMEM((levels, tracers, band, tile), f32),
        pltpu.VMEM((2, levels, band, tile), f32),
        pltpu.VMEM((levels - 1, band, tile), f32),
        pltpu.VMEM((levels, tracers, band, tile), f32),
        pltpu.VMEM((levels - 1, band, tile), f32),
        pltpu.VMEM((levels, tracers, band, tile), f32),
        pltpu.VMEM((levels * (tracers + 1), tile), f32),
        pltpu.VMEM((levels * tracers, tile), f32),
        pltpu.VMEM((tracers + 1, band, tile), f32),
        pltpu.VMEM((tracers, band, tile), f32),
        pltpu.VMEM((levels * (tracers + 1), tile), f32),
        pltpu.VMEM((levels * tracers, tile), f32),
        pltpu.VMEM((tracers + 1, band, tile), f32),
        pltpu.VMEM((tracers, band, tile), f32),
        pltpu.VMEM((tracers, 2, band, tile), f32),
        pltpu.SemaphoreType.DMA((3,)),
        pltpu.SemaphoreType.DMA((levels // 8,)),
        pltpu.SemaphoreType.DMA((4,)),
        pltpu.SemaphoreType.DMA((4,)),
    ]


def first_kernel(lon_count, lat_count, a_hbm, c_hbm, m_hbm, blocks_hbm, out_hbm, got_hbm, *scratch):
    *step, trade_send, trade_recv, own_sem = scratch
    devices = lon_count * lat_count
    me = lax.axis_index("lon") * lat_count + lax.axis_index("lat")

    def entry():
        barrier = pltpu.get_barrier_semaphore()

        @pl.loop(1, devices)
        def _(i):
            peer = lax.rem(me + i, devices)
            pl.semaphore_signal(
                barrier, inc=1, device_id={"lon": peer // lat_count, "lat": lax.rem(peer, lat_count)},
                device_id_type=MESH,
            )

        pl.semaphore_wait(barrier, devices - 1)

        @pl.loop(1, devices)
        def _(i):
            peer = lax.rem(me + i, devices)
            pltpu.make_async_remote_copy(
                src_ref=blocks_hbm.at[peer], dst_ref=got_hbm.at[me],
                send_sem=trade_send, recv_sem=trade_recv,
                device_id={"lon": peer // lat_count, "lat": lax.rem(peer, lat_count)},
                device_id_type=MESH,
            ).start()

        pltpu.make_async_copy(blocks_hbm.at[me], got_hbm.at[me], own_sem).start()

    def leave():
        pltpu.make_async_copy(blocks_hbm.at[me], got_hbm.at[me], own_sem).wait()
        most = pl.ds(0, devices - 1)
        everything = pltpu.make_async_remote_copy(
            src_ref=blocks_hbm.at[most], dst_ref=got_hbm.at[most],
            send_sem=trade_send, recv_sem=trade_recv,
            device_id={"lon": lax.axis_index("lon"), "lat": lax.rem(lax.axis_index("lat") + 1, lat_count)},
            device_id_type=MESH,
        )
        everything.wait()

    transport_body(lon_count, lat_count, entry, leave, a_hbm, c_hbm, m_hbm, out_hbm, *step)


def second_kernel(lon_count, lat_count, a_hbm, c_hbm, m_hbm, first_hbm, out_hbm, flux_ref, *scratch):
    *step, ground, ground_sem = scratch
    obuf = step[5]

    def entry():
        lon, lat = lax.axis_index("lon"), lax.axis_index("lat")
        barrier = pltpu.get_barrier_semaphore()
        for d_lon, d_lat in ((1, 0), (lon_count - 1, 0), (0, 1), (0, lat_count - 1)):
            pl.semaphore_signal(
                barrier, inc=1,
                device_id={"lon": lax.rem(lon + d_lon, lon_count), "lat": lax.rem(lat + d_lat, lat_count)},
                device_id_type=MESH,
            )
        pltpu.make_async_copy(first_hbm.at[0], ground, ground_sem).start()
        pl.semaphore_wait(barrier, 4)

    def leave():
        pltpu.make_async_copy(first_hbm.at[0], ground, ground_sem).wait()
        flux_ref[...] = ground[...] + obuf[0]

    transport_body(lon_count, lat_count, entry, leave, a_hbm, c_hbm, m_hbm, out_hbm, *step)


def first_step(state, courant, mixing, blocks, lon_count, lat_count):
    levels, tracers, band, tile = state.shape
    return pl.pallas_call(
        functools.partial(first_kernel, lon_count, lat_count),
        out_shape=(
            jax.ShapeDtypeStruct(state.shape, jnp.float32),
            jax.ShapeDtypeStruct(blocks.shape, jnp.float32),
        ),
        in_specs=[ANY] * 4,
        out_specs=(ANY, ANY),
        scratch_shapes=step_scratch(levels, tracers, band, tile)
        + [pltpu.SemaphoreType.DMA, pltpu.SemaphoreType.DMA, pltpu.SemaphoreType.DMA],
        compiler_params=pltpu.CompilerParams(
            collective_id=0, has_side_effects=True, vmem_limit_bytes=VMEM_LIMIT
        ),
        name="first_step",
    )(state, courant, mixing, blocks)


def second_step(state, courant, mixing, after_first, lon_count, lat_count):
    levels, tracers, band, tile = state.shape
    return pl.pallas_call(
        functools.partial(second_kernel, lon_count, lat_count),
        out_shape=(
            jax.ShapeDtypeStruct(state.shape, jnp.float32),
            jax.ShapeDtypeStruct(state.shape[1:], jnp.float32),
        ),
        in_specs=[ANY] * 4,
        out_specs=(ANY, pl.BlockSpec(memory_space=pltpu.VMEM)),
        scratch_shapes=step_scratch(levels, tracers, band, tile)
        + [pltpu.VMEM((tracers, band, tile), jnp.float32), pltpu.SemaphoreType.DMA],
        compiler_params=pltpu.CompilerParams(
            collective_id=1, has_side_effects=True, vmem_limit_bytes=VMEM_LIMIT
        ),
        name="second_step",
    )(state, courant, mixing, after_first)


def force_kernel(capacity, levels, lines, got_ref, state_hbm, out_hbm, rows, ids, ids_smem, state, *rest):
    sums, (ids_sem, load_sem, store_sem) = rest[:STREAMS], rest[STREAMS:]
    devices = got_ref.shape[0]
    cells_all = lines * LANES
    load = pltpu.make_async_copy(state_hbm, state, load_sem)
    load.start()
    low = lane_iota((HALF, LANES)) < capacity

    @pl.loop(0, devices // 2)
    def _(pair):
        one, two = got_ref[2 * pair], got_ref[2 * pair + 1]
        first = jnp.where(low, one, pltpu.roll(two, capacity, 1))
        second = jnp.where(low, pltpu.roll(one, capacity, 1), two)
        cell = second[levels - HALF : levels - HALF + 1, :].astype(jnp.int32)
        ids[pl.ds(pair, 1), :] = jnp.where(cell < 0, cells_all, cell)
        wide = jnp.concatenate([first, second, jnp.zeros((LANES - 2 * HALF, LANES), jnp.float32)], axis=0)
        rows[pl.ds(pl.multiple_of(pair * LANES, LANES), LANES), :] = wide.T

    to_smem = pltpu.make_async_copy(ids, ids_smem, ids_sem)
    to_smem.start()
    zero = jnp.zeros((64, LANES), jnp.float32)

    @pl.loop(0, cells_all // 64)
    def _(i):
        for s in range(STREAMS):
            sums[s][pl.ds(pl.multiple_of(i * 64, 64), 64), :] = zero

    to_smem.wait()

    @pl.loop(0, devices // 2)
    def _(pair):
        @pl.loop(0, LANES // (4 * STREAMS))
        def _(part):
            for i in range(4):
                at = [part * 4 * STREAMS + i * STREAMS + s for s in range(STREAMS)]
                cell = [ids_smem[pair, at[s]] for s in range(STREAMS)]
                new = [
                    sums[s][pl.ds(cell[s], 1), :] + rows[pl.ds(pair * LANES + at[s], 1), :]
                    for s in range(STREAMS)
                ]
                for s in range(STREAMS):
                    sums[s][pl.ds(cell[s], 1), :] = new[s]

    load.wait()

    @pl.loop(0, cells_all // LANES)
    def _(line):
        span = pl.ds(pl.multiple_of(line * LANES, LANES), LANES)
        total = sums[0][span, :]
        for s in range(1, STREAMS):
            total = total + sums[s][span, :]
        at = pl.ds(line, levels, stride=cells_all // LANES)
        state[at, :] = state[at, :] + total.T[:levels]

    store = pltpu.make_async_copy(state, out_hbm, store_sem)
    store.start()
    store.wait()


def add_forcing(got, after_first, capacity):
    levels, tracers, band, tile = after_first.shape
    devices = got.shape[0]
    lines = tracers * band
    flat = after_first.reshape(levels * lines, tile)

    out = pl.pallas_call(
        functools.partial(force_kernel, capacity, levels, lines),
        out_shape=jax.ShapeDtypeStruct(flat.shape, jnp.float32),
        in_specs=[pl.BlockSpec(memory_space=pltpu.VMEM), ANY],
        out_specs=ANY,
        scratch_shapes=[
            pltpu.VMEM((devices * capacity, LANES), jnp.float32),
            pltpu.VMEM((devices // 2, LANES), jnp.int32),
            pltpu.SMEM((devices // 2, LANES), jnp.int32),
            pltpu.VMEM(flat.shape, jnp.float32),
        ]
        + [pltpu.VMEM((lines * tile + 8, LANES), jnp.float32)] * STREAMS
        + [pltpu.SemaphoreType.DMA] * 3,
        compiler_params=pltpu.CompilerParams(vmem_limit_bytes=VMEM_LIMIT),
        name="add_forcing",
    )(got, flat)
    return out.reshape(after_first.shape)


def on_device(adjoint_in, courant, mixing, kernel_blocks, sounding_dest, sounding_cell):
    lon_count = lax.axis_size("lon")
    lat_count = lax.axis_size("lat")
    devices = lon_count * lat_count
    held = kernel_blocks.shape[1]
    capacity = 4 * held // devices
    owner = sounding_dest.reshape(held // LANES, LANES)
    cell = sounding_cell.reshape(held // LANES, LANES)
    blocks = pack(kernel_blocks, owner, cell, devices, capacity)
    after_first, got = first_step(adjoint_in, courant, mixing, blocks, lon_count, lat_count)
    forced = add_forcing(got, after_first, capacity)
    return second_step(forced, courant, mixing, after_first, lon_count, lat_count)


def solution(mesh):
    placed = (
        P(None, None, "lat", "lon"),
        P(None, None, "lat", "lon"),
        P(None, "lat", "lon"),
        P(None, ("lon", "lat")),
        P(("lon", "lat"), None),
        P(("lon", "lat")),
    )
    return jax.shard_map(
        on_device,
        mesh=mesh,
        in_specs=placed,
        out_specs=(P(None, None, "lat", "lon"), P(None, "lat", "lon")),
        check_vma=False,
    )
```

profile of v0, /device:TPU:67, one launch (start us, length us, event | category | flops | bytes accessed | tf_op | source)
XLA Modules:
  0.0 197.5 jit_solution(16762811516521030537)
XLA Ops:
  0.6 19.2 %pack_soundings.1.blocks_hbm = f32[128,40,128]{2,1,0:T(8,128)} custom-call(f32[72,2048]{1,0:T(8,128)} %blocks_ref.1, s32[16,128]{1,0:T(8,128)} %bitcast.6, s32[16,128]{1,0:T(8,128)} %bitcast.7), custom_call_target="tpu_custom_call" | custom-call | tf_op jit(solution)/shard_map/pack_soundings/pallas_call | solution.py:81
  19.8 75.2 %first_step.1 = (f32[72,2,64,128]{3,2,1,0:T(8,128)}, f32[128,40,128]{2,1,0:T(8,128)}) custom-call(f32[72,2,64,128]{3,2,1,0:T(8,128)} %a_hbm.1, f32[2,72,64,128]{3,2,1,0:T(8,128)} %c_hbm.3, f32[71,64,128]{2,1,0:T(8,128)} %m_hbm.3, f32[128,40,128]{2,1,0:T(8,128)} %pack_soundings.1.blocks_hbm), custom_call_target="tpu_custom_call" | custom-call | tf_op jit(solution)/shard_map/first_step/pallas_call | solution.py:381
  95.1 53.6 %add_forcing.1 = f32[9216,128]{1,0:T(8,128)} custom-call(f32[128,40,128]{2,1,0:T(8,128)} %get-tuple-element.4.got_ref, f32[9216,128]{1,0:T(8,128)} %bitcast.4), custom_call_target="tpu_custom_call" | custom-call | tf_op jit(solution)/shard_map/add_forcing/pallas_call | solution.py:482
  148.7 42.9 %second_step.1 = (f32[72,2,64,128]{3,2,1,0:T(8,128)}, f32[2,64,128]{2,1,0:T(8,128)}) custom-call(f32[72,2,64,128]{3,2,1,0:T(8,128)} %bitcast.5, f32[2,72,64,128]{3,2,1,0:T(8,128)} %c_hbm.3, f32[71,64,128]{2,1,0:T(8,128)} %m_hbm.3, f32[72,2,64,128]{3,2,1,0:T(8,128)} %get-tuple-element.5.first_hbm), custom_call_target="tpu_custom_call" | custom-call | tf_op jit(solution)/shard_map/second_step/pallas_call | solution.py:400
  191.6 0.0 copy-start
  191.6 5.3 %copy.10 = f32[72,2,64,128]{3,2,1,0:T(8,128)} copy(f32[72,2,64,128]{3,2,1,0:T(8,128)} %get-tuple-element.8) | data formatting | bytes 9437184
  196.8 0.0 copy-done
  196.8 0.6 copy.11
Async XLA Ops:
  191.6 5.3 %copy-start = (f32[2,64,128]{2,1,0:T(8,128)S(1)}, f32[2,64,128]{2,1,0:T(8,128)}, u32[]{:S(2)}) copy-start(f32[2,64,128]{2,1,0:T(8,128)} %get-tuple-element.9) | copy-start | bytes 196612
where the time goes:
time: 198 us; the launch traced here: 197 us
  Pallas kernels  191 us (96%)
  local copies, waits for them, and re-layouts  5.91 us (3%)
    pallas_call x1, Pallas kernels, first_step(): pl.pallas_call(functools.partial(first_kernel, lon_count, lat_count), out...  75.2 us
    pallas_call x1, Pallas kernels, add_forcing(): pl.pallas_call(functools.partial(force_kernel, capacity, levels, lines),...  53.6 us
    pallas_call x1, Pallas kernels, second_step(): pl.pallas_call(functools.partial(second_kernel, lon_count, lat_count), ou...  42.9 us
    pallas_call x1, Pallas kernels, pack(): pl.pallas_call(functools.partial(pack_kernel, devices, capacity, levels),...  19.2 us
    unnamed x4, local copies, waits for them, and re-layouts  5.91 us

commit v1 on v0

v1 whole, which is shorter than its diff:
```python
import functools
import jax
import jax.numpy as jnp
from jax import lax
from jax.experimental import pallas as pl
from jax.experimental.pallas import tpu as pltpu
from jax.sharding import PartitionSpec as P

MESH = pl.DeviceIdType.MESH
ANY = pl.BlockSpec(memory_space=pl.ANY)
LANES = 128
HALF = 40
STREAMS = 4
VMEM_LIMIT = 60 * 1024 * 1024


def lane_iota(shape):
    return lax.broadcasted_iota(jnp.int32, shape, len(shape) - 1)


def pack_kernel(
    devices, capacity, levels, blocks_ref, dest_ref, cell_ref, out_ref, rows, slots, order, order_smem, sems
):
    held = blocks_ref.shape[1]
    chunks = held // LANES
    row_id = lax.broadcasted_iota(jnp.int32, (LANES, LANES), 0)
    col_id = lax.broadcasted_iota(jnp.int32, (LANES, LANES), 1)
    before = jnp.where(row_id < col_id, 1.0, 0.0).astype(jnp.bfloat16)
    ones = jnp.ones((LANES, LANES), jnp.bfloat16)
    base = jnp.zeros((LANES, LANES), jnp.float32)

    def to_smem(chunk):
        return pltpu.make_async_copy(
            order.at[chunk], order_smem.at[pl.ds(chunk * LANES, LANES)], sems.at[chunk]
        )

    for chunk in range(chunks):
        owner = dest_ref[chunk : chunk + 1, :]
        hot = jnp.broadcast_to(owner, (LANES, LANES)) == row_id
        hot_f = jnp.where(hot, 1.0, 0.0)
        hot_b = hot_f.astype(jnp.bfloat16)
        earlier = jnp.dot(hot_b, before, preferred_element_type=jnp.float32)
        rank = jnp.sum(hot_f * (earlier + base), axis=0, keepdims=True)
        order[chunk : chunk + 1, :] = owner * capacity + rank.astype(jnp.int32)
        base = base + jnp.dot(hot_b, ones, preferred_element_type=jnp.float32)
    for chunk in range(chunks):
        to_smem(chunk).start()
    blank = jnp.where(lane_iota((64, LANES)) == levels, -1.0, 0.0)

    @pl.loop(0, devices * capacity // 64)
    def _(i):
        slots[pl.ds(pl.multiple_of(i * 64, 64), 64), :] = blank

    for chunk in range(chunks):
        span = slice(chunk * LANES, (chunk + 1) * LANES)
        tall = jnp.concatenate(
            [
                blocks_ref[:, span],
                jnp.broadcast_to(cell_ref[chunk : chunk + 1, :].astype(jnp.float32), (8, LANES)),
                jnp.zeros((LANES - levels - 8, LANES), jnp.float32),
            ],
            axis=0,
        )
        rows[span, :] = tall.T
    for chunk in range(chunks):
        to_smem(chunk).wait()

    @pl.loop(0, held // 16)
    def _(part):
        for i in range(16):
            at = part * 16 + i
            slots[pl.ds(order_smem[at], 1), :] = rows[pl.ds(at, 1), :]

    low = lane_iota((HALF, LANES)) < capacity
    group = 8

    @pl.loop(0, devices // (2 * group))
    def _(part):
        wides = []
        for i in range(group):
            at = pl.multiple_of((part * group + i) * LANES, LANES)
            wides.append(slots[pl.ds(at, LANES), :].T)
        for i, wide in enumerate(wides):
            first, second = wide[:HALF], wide[HALF : 2 * HALF]
            pair = part * group + i
            out_ref[2 * pair] = jnp.where(low, first, pltpu.roll(second, capacity, 1))
            out_ref[2 * pair + 1] = jnp.where(low, pltpu.roll(first, capacity, 1), second)


def pack(kernel_blocks, owner, cell, devices, capacity):
    levels, held = kernel_blocks.shape
    return pl.pallas_call(
        functools.partial(pack_kernel, devices, capacity, levels),
        out_shape=jax.ShapeDtypeStruct((devices, HALF, LANES), jnp.float32),
        in_specs=[pl.BlockSpec(memory_space=pltpu.VMEM)] * 3,
        out_specs=pl.BlockSpec(memory_space=pltpu.VMEM),
        scratch_shapes=[
            pltpu.VMEM((held, LANES), jnp.float32),
            pltpu.VMEM((devices * capacity, LANES), jnp.float32),
            pltpu.VMEM((held // LANES, LANES), jnp.int32),
            pltpu.SMEM((held,), jnp.int32),
            pltpu.SemaphoreType.DMA((held // LANES,)),
        ],
        compiler_params=pltpu.CompilerParams(vmem_limit_bytes=VMEM_LIMIT),
        name="pack_soundings",
    )(kernel_blocks, owner, cell)


def transport_front(lon_count, lat_count, hooks, a_hbm, c_hbm, m_hbm, front):
    (
        a_ref, c_ref, m_ref, vbuf, rbuf, send_n, send_s, send_e, send_w,
        from_s, from_n, from_w, from_e, rows_fix, merged, load_sem, send_sem, recv_sem,
    ) = front
    at_entry, after_rows, after_columns, during_columns = hooks
    levels, tracers, band, tile = a_ref.shape
    lon, lat = lax.axis_index("lon"), lax.axis_index("lat")
    north = {"lon": lon, "lat": lax.rem(lat + 1, lat_count)}
    south = {"lon": lon, "lat": lax.rem(lat + lat_count - 1, lat_count)}
    east = {"lon": lax.rem(lon + 1, lon_count), "lat": lat}
    west = {"lon": lax.rem(lon + lon_count - 1, lon_count), "lat": lat}

    loads = [
        pltpu.make_async_copy(m_hbm, m_ref, load_sem.at[0]),
        pltpu.make_async_copy(a_hbm, a_ref, load_sem.at[1]),
        pltpu.make_async_copy(c_hbm, c_ref, load_sem.at[2]),
    ]
    for load in loads:
        load.start()
    at_entry()
    loads[0].wait()
    loads[1].wait()

    mix = m_ref[0]
    inverse = 1.0 / (1.0 + mix)
    ratio = mix * inverse
    solved = a_ref[0] * inverse[None]
    rbuf[0] = ratio
    vbuf[0] = solved

    def down(k, carry):
        mix_above, ratio, solved = carry
        mix = m_ref[k]
        inverse = 1.0 / (1.0 + mix_above + mix - mix_above * ratio)
        ratio = mix * inverse
        solved = (a_ref[k] + mix_above[None] * solved) * inverse[None]
        rbuf[k] = ratio
        vbuf[k] = solved
        return mix, ratio, solved

    mix, ratio, solved = lax.fori_loop(1, levels - 1, down, (mix, ratio, solved))
    inverse = 1.0 / (1.0 + mix - mix * ratio)
    solved = (a_ref[levels - 1] + mix[None] * solved) * inverse[None]

    def keep(k, solved):
        vbuf[k] = solved
        for t in range(tracers):
            send_s[pl.ds(t * levels + k, 1), :] = solved[t, 0:1, :]
            send_n[pl.ds(t * levels + k, 1), :] = solved[t, band - 1 : band, :]

    keep(levels - 1, solved)

    def up(i, solved):
        k = levels - 2 - i
        solved = vbuf[k] + rbuf[k][None] * solved
        keep(k, solved)
        return solved

    lax.fori_loop(0, levels - 1, up, solved)

    loads[2].wait()
    edge = jnp.where(lat == lat_count - 1, 0.0, 1.0)

    @pl.loop(0, levels // 8)
    def _(j):
        for i in range(8):
            k = j * 8 + i
            send_n[pl.ds(tracers * levels + k, 1), :] = c_ref[1, k, band - 1 : band, :] * edge

    def remote(index, src, dst, to):
        return pltpu.make_async_remote_copy(
            src_ref=src, dst_ref=dst, send_sem=send_sem.at[index], recv_sem=recv_sem.at[index],
            device_id=to, device_id_type=MESH,
        )

    to_north = remote(0, send_n, from_s, north)
    to_south = remote(1, send_s, from_n, south)
    to_north.start()
    to_south.start()
    after_rows()

    top = lax.broadcasted_iota(jnp.int32, (band, tile), 0) == band - 1

    @pl.loop(0, levels // 2)
    def _(j):
        swept = []
        for i in range(2):
            face = c_ref[1, 2 * j + i]
            out_face, in_face = jnp.maximum(face, 0.0), jnp.minimum(face, 0.0)
            for t in range(tracers):
                cells = vbuf[2 * j + i, t]
                rise = jnp.where(top, 0.0, pltpu.roll(cells, band - 1, 0) - cells)
                swept.append(cells + out_face * rise + pltpu.roll(in_face * rise, 1, 0))
        for i in range(2):
            for t in range(tracers):
                vbuf[2 * j + i, t] = swept[tracers * i + t]

    lane = lane_iota((8, tile))
    zero = jnp.zeros((8, tile), jnp.float32)

    @pl.loop(0, band // 8)
    def _(g):
        span = pl.ds(pl.multiple_of(g * 8, 8), 8)
        last = zero
        for k in range(levels):
            last = jnp.where(lane == (k - 1) % tile, pltpu.roll(c_ref[0, k, span, :], k, 1), last)
        send_e[tracers, span, :] = last

    to_north.wait()
    to_south.wait()
    face_south = jnp.minimum(from_s[tracers * levels :, :], 0.0)
    face_north = jnp.maximum(send_n[tracers * levels :, :], 0.0)
    for t in range(tracers):
        part = slice(t * levels, (t + 1) * levels)
        rows_fix[part, :] = face_south * (send_s[part, :] - from_s[part, :])
        rows_fix[tracers * levels + t * levels : tracers * levels + (t + 1) * levels, :] = face_north * (
            from_n[part, :] - send_n[part, :]
        )

    row = lax.broadcasted_iota(jnp.int32, (8, tile), 0)

    def columns(g, fixed, at):
        span = pl.ds(pl.multiple_of(g * 8, 8), 8)
        for t in range(tracers):
            first, last = zero, zero
            for k in range(levels):
                cells = vbuf[k, t, span, :]
                if fixed is not None:
                    fix = rows_fix[fixed + t * levels + k : fixed + t * levels + k + 1, :]
                    cells = cells + jnp.where(row == at, jnp.broadcast_to(fix, (8, tile)), 0.0)
                    vbuf[k, t, span, :] = cells
                turned = pltpu.roll(cells, k, 1)
                first = jnp.where(lane == k, turned, first)
                last = jnp.where(lane == (k - 1) % tile, turned, last)
            send_w[t, span, :] = first
            send_e[t, span, :] = last

    columns(0, 0, 0)
    columns(band // 8 - 1, tracers * levels, 7)

    @pl.loop(1, band // 8 - 1)
    def _(g):
        columns(g, None, None)

    to_east = remote(2, send_e, from_w, east)
    to_west = remote(3, send_w, from_e, west)
    to_east.start()
    to_west.start()
    after_columns()
    during_columns()
    to_east.wait()
    to_west.wait()

    even = lax.rem(lane_iota((band, tile)), 2) == 0
    face_last = jnp.maximum(pltpu.roll(send_e[tracers], 1, 1), 0.0)
    face_first = jnp.minimum(pltpu.roll(from_w[tracers], 2, 1), 0.0)
    for t in range(tracers):
        at_last = face_last * (from_e[t] - pltpu.roll(send_e[t], 1, 1))
        at_first = face_first * (pltpu.roll(send_w[t], 1, 1) - pltpu.roll(from_w[t], 2, 1))
        merged[t, 0] = jnp.where(even, at_last, at_first)
        merged[t, 1] = jnp.where(even, at_first, at_last)


def front_scratch(levels, tracers, band, tile, merged=True):
    f32 = jnp.float32
    return [
        pltpu.VMEM((levels, tracers, band, tile), f32),
        pltpu.VMEM((2, levels, band, tile), f32),
        pltpu.VMEM((levels - 1, band, tile), f32),
        pltpu.VMEM((levels, tracers, band, tile), f32),
        pltpu.VMEM((levels - 1, band, tile), f32),
        pltpu.VMEM((levels * (tracers + 1), tile), f32),
        pltpu.VMEM((levels * tracers, tile), f32),
        pltpu.VMEM((tracers + 1, band, tile), f32),
        pltpu.VMEM((tracers, band, tile), f32),
        pltpu.VMEM((levels * (tracers + 1), tile), f32),
        pltpu.VMEM((levels * tracers, tile), f32),
        pltpu.VMEM((tracers + 1, band, tile), f32),
        pltpu.VMEM((tracers, band, tile), f32),
        pltpu.VMEM((2 * tracers * levels, tile), f32),
        pltpu.VMEM((tracers, 2, band, tile), f32),
        pltpu.SemaphoreType.DMA((3,)),
        pltpu.SemaphoreType.DMA((4,)),
        pltpu.SemaphoreType.DMA((4,)),
    ]


FRONT = 18


def sweep_columns(levels, tracers, lane, load_face, load_cells, load_sides, store):
    tile = lane.shape[1]
    for k in range(levels):
        face = load_face(k)
        out_face, in_face = jnp.maximum(face, 0.0), jnp.minimum(face, 0.0)
        for t in range(tracers):
            cells = load_cells(k, t)
            rise = jnp.where(lane == tile - 1, 0.0, pltpu.roll(cells, tile - 1, 1) - cells)
            swept = cells + out_face * rise + pltpu.roll(in_face * rise, 1, 1)
            if load_sides is not None:
                swept = swept + sides_of(lane, load_sides(k, t), k)
            store(k, t, swept)


def sides_of(lane, merged, k):
    tile = lane.shape[1]
    return jnp.where((lane == 0) | (lane == tile - 1), pltpu.roll(merged, tile - 1 - k, 1), 0.0)


def first_kernel(lon_count, lat_count, a_hbm, c_hbm, m_hbm, blocks_hbm, out_hbm, got_hbm, *scratch):
    front, (obuf, store_sem, trade_send, trade_recv, own_sem) = scratch[:FRONT], scratch[FRONT:]
    c_ref, vbuf, merged = front[1], front[3], front[14]
    levels, tracers, band, tile = vbuf.shape
    devices = lon_count * lat_count
    me = lax.axis_index("lon") * lat_count + lax.axis_index("lat")

    def trade(begin, end):
        @pl.loop(begin, end)
        def _(i):
            peer = lax.rem(me + i, devices)
            pltpu.make_async_remote_copy(
                src_ref=blocks_hbm.at[peer], dst_ref=got_hbm.at[me],
                send_sem=trade_send, recv_sem=trade_recv,
                device_id={"lon": peer // lat_count, "lat": lax.rem(peer, lat_count)},
                device_id_type=MESH,
            ).start()

    cuts = (1, 1 + devices // 4, devices // 2, devices)

    def at_entry():
        barrier = pltpu.get_barrier_semaphore()

        @pl.loop(1, devices)
        def _(i):
            peer = lax.rem(me + i, devices)
            pl.semaphore_signal(
                barrier, inc=1, device_id={"lon": peer // lat_count, "lat": lax.rem(peer, lat_count)},
                device_id_type=MESH,
            )

        pl.semaphore_wait(barrier, devices - 1)
        trade(cuts[0], cuts[1])
        pltpu.make_async_copy(blocks_hbm.at[me], got_hbm.at[me], own_sem).start()

    lane = lane_iota((8, tile))

    def main_sweep():
        @pl.loop(0, band // 8)
        def _(g):
            span = pl.ds(pl.multiple_of(g * 8, 8), 8)

            def store(k, t, swept):
                obuf[k, t, span, :] = swept

            sweep_columns(
                levels, tracers, lane, lambda k: c_ref[0, k, span, :],
                lambda k, t: vbuf[k, t, span, :], None, store,
            )

    hooks = (at_entry, lambda: trade(cuts[1], cuts[2]), lambda: trade(cuts[2], cuts[3]), main_sweep)
    transport_front(lon_count, lat_count, hooks, a_hbm, c_hbm, m_hbm, front)

    def stored(g):
        span = pl.ds(pl.multiple_of(g * 8, 8), 8)
        return pltpu.make_async_copy(obuf.at[:, :, span, :], out_hbm.at[:, :, span, :], store_sem.at[g])

    @pl.loop(0, band // 8)
    def _(g):
        span = pl.ds(pl.multiple_of(g * 8, 8), 8)
        for t in range(tracers):
            sides = [merged[t, 0, span, :], merged[t, 1, span, :]]
            for k in range(levels):
                obuf[k, t, span, :] = obuf[k, t, span, :] + sides_of(lane, sides[k % 2], k)
        stored(g).start()

    pltpu.make_async_copy(blocks_hbm.at[me], got_hbm.at[me], own_sem).wait()
    most = pl.ds(0, devices - 1)
    pltpu.make_async_remote_copy(
        src_ref=blocks_hbm.at[most], dst_ref=got_hbm.at[most],
        send_sem=trade_send, recv_sem=trade_recv,
        device_id={"lon": lax.axis_index("lon"), "lat": lax.rem(lax.axis_index("lat") + 1, lat_count)},
        device_id_type=MESH,
    ).wait()

    @pl.loop(0, band // 8)
    def _(g):
        stored(g).wait()


def second_kernel(lon_count, lat_count, a_hbm, c_hbm, m_hbm, out_hbm, sides_ref, *scratch):
    front, (store_sem,) = scratch[:FRONT], scratch[FRONT:]
    vbuf, merged = front[3], front[14]

    def at_entry():
        lon, lat = lax.axis_index("lon"), lax.axis_index("lat")
        barrier = pltpu.get_barrier_semaphore()
        for d_lon, d_lat in ((1, 0), (lon_count - 1, 0), (0, 1), (0, lat_count - 1)):
            pl.semaphore_signal(
                barrier, inc=1,
                device_id={"lon": lax.rem(lon + d_lon, lon_count), "lat": lax.rem(lat + d_lat, lat_count)},
                device_id_type=MESH,
            )
        pl.semaphore_wait(barrier, 4)

    store = pltpu.make_async_copy(vbuf, out_hbm, store_sem)
    hooks = (at_entry, lambda: None, store.start, lambda: None)
    transport_front(lon_count, lat_count, hooks, a_hbm, c_hbm, m_hbm, front)
    sides_ref[...] = merged[...]
    store.wait()


def first_step(state, courant, mixing, blocks, lon_count, lat_count):
    levels, tracers, band, tile = state.shape
    return pl.pallas_call(
        functools.partial(first_kernel, lon_count, lat_count),
        out_shape=(
            jax.ShapeDtypeStruct(state.shape, jnp.float32),
            jax.ShapeDtypeStruct(blocks.shape, jnp.float32),
        ),
        in_specs=[ANY] * 4,
        out_specs=(ANY, ANY),
        scratch_shapes=front_scratch(levels, tracers, band, tile)
        + [
            pltpu.VMEM((levels, tracers, band, tile), jnp.float32),
            pltpu.SemaphoreType.DMA((band // 8,)),
            pltpu.SemaphoreType.DMA,
            pltpu.SemaphoreType.DMA,
            pltpu.SemaphoreType.DMA,
        ],
        compiler_params=pltpu.CompilerParams(
            collective_id=0, has_side_effects=True, vmem_limit_bytes=VMEM_LIMIT
        ),
        name="first_step",
    )(state, courant, mixing, blocks)


def second_front(state, courant, mixing, lon_count, lat_count):
    levels, tracers, band, tile = state.shape
    return pl.pallas_call(
        functools.partial(second_kernel, lon_count, lat_count),
        out_shape=(
            jax.ShapeDtypeStruct(state.shape, jnp.float32),
            jax.ShapeDtypeStruct((tracers, 2, band, tile), jnp.float32),
        ),
        in_specs=[ANY] * 3,
        out_specs=(ANY, pl.BlockSpec(memory_space=pltpu.VMEM)),
        scratch_shapes=front_scratch(levels, tracers, band, tile) + [pltpu.SemaphoreType.DMA],
        compiler_params=pltpu.CompilerParams(
            collective_id=1, has_side_effects=True, vmem_limit_bytes=VMEM_LIMIT
        ),
        name="second_front",
    )(state, courant, mixing)


def last_kernel(cells_ref, face_ref, sides_ref, ground_ref, out_ref, flux_ref):
    levels, tracers, _, tile = cells_ref.shape
    lane = lane_iota((8, tile))
    sides = [[sides_ref[t, p] for p in range(2)] for t in range(tracers)]

    def store(k, t, swept):
        out_ref[k, t] = swept
        if k == 0:
            flux_ref[t] = ground_ref[0, t] + swept

    sweep_columns(
        levels, tracers, lane, lambda k: face_ref[0, k], lambda k, t: cells_ref[k, t],
        lambda k, t: sides[t][k % 2], store,
    )


def last_sweep(cells, courant, sides, after_first):
    levels, tracers, band, tile = cells.shape
    return pl.pallas_call(
        last_kernel,
        grid=(band // 8,),
        out_shape=(
            jax.ShapeDtypeStruct(cells.shape, jnp.float32),
            jax.ShapeDtypeStruct(cells.shape[1:], jnp.float32),
        ),
        in_specs=[
            pl.BlockSpec((levels, tracers, 8, tile), lambda g: (0, 0, g, 0)),
            pl.BlockSpec((1, levels, 8, tile), lambda g: (0, 0, g, 0)),
            pl.BlockSpec((tracers, 2, 8, tile), lambda g: (0, 0, g, 0)),
            pl.BlockSpec((1, tracers, 8, tile), lambda g: (0, 0, g, 0)),
        ],
        out_specs=(
            pl.BlockSpec((levels, tracers, 8, tile), lambda g: (0, 0, g, 0)),
            pl.BlockSpec((tracers, 8, tile), lambda g: (0, g, 0)),
        ),
        compiler_params=pltpu.CompilerParams(vmem_limit_bytes=VMEM_LIMIT),
        name="last_sweep",
    )(cells, courant, sides, after_first)


def force_kernel(capacity, levels, lines, got_ref, state_hbm, out_hbm, rows, ids, ids_smem, state, total, *rest):
    sums, (ids_sem, load_sem, store_sem) = rest[:STREAMS], rest[STREAMS:]
    devices = got_ref.shape[0]
    cells_all = lines * LANES
    load = pltpu.make_async_copy(state_hbm, state, load_sem)
    load.start()
    low = lane_iota((HALF, LANES)) < capacity
    group = 8

    def to_smem(pair):
        return pltpu.make_async_copy(
            ids.at[pair], ids_smem.at[pl.ds(pair * LANES, LANES)], ids_sem.at[pair]
        )

    @pl.loop(0, devices // (2 * group))
    def _(part):
        for i in range(group):
            pair = part * group + i
            one, two = got_ref[2 * pair], got_ref[2 * pair + 1]
            first = jnp.where(low, one, pltpu.roll(two, capacity, 1))
            second = jnp.where(low, pltpu.roll(one, capacity, 1), two)
            cell = second[levels - HALF : levels - HALF + 1, :].astype(jnp.int32)
            ids[pl.ds(pair, 1), :] = jnp.where(cell < 0, cells_all, cell)
            wide = jnp.concatenate([first, second, jnp.zeros((LANES - 2 * HALF, LANES), jnp.float32)], axis=0)
            rows[pl.ds(pl.multiple_of(pair * LANES, LANES), LANES), :] = wide.T

    @pl.loop(0, devices // 2)
    def _(pair):
        to_smem(pair).start()

    zero = jnp.zeros((64, LANES), jnp.float32)

    @pl.loop(0, cells_all // 64)
    def _(i):
        for s in range(STREAMS):
            sums[s][pl.ds(pl.multiple_of(i * 64, 64), 64), :] = zero

    @pl.loop(0, devices // 2)
    def _(pair):
        to_smem(pair).wait()

    @pl.loop(0, devices * capacity // (4 * STREAMS))
    def _(part):
        for i in range(4):
            at = [part * 4 * STREAMS + i * STREAMS + s for s in range(STREAMS)]
            cell = [ids_smem[at[s]] for s in range(STREAMS)]
            new = [sums[s][pl.ds(cell[s], 1), :] + rows[pl.ds(at[s], 1), :] for s in range(STREAMS)]
            for s in range(STREAMS):
                sums[s][pl.ds(cell[s], 1), :] = new[s]

    load.wait()

    def stored(part):
        span = pl.ds(pl.multiple_of(part * group, group), group)
        return pltpu.make_async_copy(
            total.reshape(levels, lines, LANES).at[:, span, :], out_hbm.at[:, span, :], store_sem.at[part]
        )

    @pl.loop(0, lines // group)
    def _(part):
        turned = []
        for i in range(group):
            span = pl.ds(pl.multiple_of((part * group + i) * LANES, LANES), LANES)
            total_here = sums[0][span, :]
            for s in range(1, STREAMS):
                total_here = total_here + sums[s][span, :]
            turned.append(total_here.T[:levels])
        for i in range(group):
            at = pl.ds(part * group + i, levels, stride=lines)
            total[at, :] = state[at, :] + turned[i]
        stored(part).start()

    @pl.loop(0, lines // group)
    def _(part):
        stored(part).wait()


def add_forcing(got, after_first, capacity):
    levels, tracers, band, tile = after_first.shape
    devices = got.shape[0]
    lines = tracers * band
    out = pl.pallas_call(
        functools.partial(force_kernel, capacity, levels, lines),
        out_shape=jax.ShapeDtypeStruct((levels, lines, tile), jnp.float32),
        in_specs=[pl.BlockSpec(memory_space=pltpu.VMEM), ANY],
        out_specs=ANY,
        scratch_shapes=[
            pltpu.VMEM((devices * capacity, LANES), jnp.float32),
            pltpu.VMEM((devices // 2, LANES), jnp.int32),
            pltpu.SMEM((devices * capacity,), jnp.int32),
            pltpu.VMEM((levels * lines, tile), jnp.float32),
            pltpu.VMEM((levels * lines, tile), jnp.float32),
        ]
        + [pltpu.VMEM((lines * tile + 8, LANES), jnp.float32)] * STREAMS
        + [
            pltpu.SemaphoreType.DMA((devices // 2,)),
            pltpu.SemaphoreType.DMA,
            pltpu.SemaphoreType.DMA((lines // 8,)),
        ],
        compiler_params=pltpu.CompilerParams(vmem_limit_bytes=VMEM_LIMIT),
        name="add_forcing",
    )(got, after_first.reshape(levels * lines, tile))
    return out.reshape(after_first.shape)


def on_device(adjoint_in, courant, mixing, kernel_blocks, sounding_dest, sounding_cell):
    lon_count = lax.axis_size("lon")
    lat_count = lax.axis_size("lat")
    devices = lon_count * lat_count
    held = kernel_blocks.shape[1]
    capacity = 4 * held // devices
    owner = sounding_dest.reshape(held // LANES, LANES)
    cell = sounding_cell.reshape(held // LANES, LANES)
    blocks = pack(kernel_blocks, owner, cell, devices, capacity)
    after_first, got = first_step(adjoint_in, courant, mixing, blocks, lon_count, lat_count)
    forced = add_forcing(got, after_first, capacity)
    swept, sides = second_front(forced, courant, mixing, lon_count, lat_count)
    return last_sweep(swept, courant, sides, after_first)


def solution(mesh):
    placed = (
        P(None, None, "lat", "lon"),
        P(None, None, "lat", "lon"),
        P(None, "lat", "lon"),
        P(None, ("lon", "lat")),
        P(("lon", "lat"), None),
        P(("lon", "lat")),
    )
    return jax.shard_map(
        on_device,
        mesh=mesh,
        in_specs=placed,
        out_specs=(P(None, None, "lat", "lon"), P(None, "lat", "lon")),
        check_vma=False,
    )
```

time: 198 us -> 200 us (1.010)
  the two profiles are of different devices: /device:TPU:67 before, /device:TPU:6 now
where the time goes in v1:
time: 200 us
  Pallas kernels  199 us (100%)
    pallas_call x1, Pallas kernels, first_step(): pl.pallas_call(functools.partial(first_kernel, lon_count, lat_count), out...  76.9 us
    pallas_call x1, Pallas kernels, last_sweep(): pl.pallas_call(last_kernel, grid=(band // 8,), out_shape=(jax.ShapeDtypeS...  60.6 us
    pallas_call x1, Pallas kernels, add_forcing(): pl.pallas_call(functools.partial(force_kernel, capacity, levels, lines),...  30.8 us
    pallas_call x1, Pallas kernels, second_front(): pl.pallas_call(functools.partial(second_kernel, lon_count, lat_count), ou...  21.6 us
    pallas_call x1, Pallas kernels, pack(): pl.pallas_call(functools.partial(pack_kernel, devices, capacity, levels),...  9.01 us

profile of v1, /device:TPU:6, one launch (start us, length us, event | category | flops | bytes accessed | tf_op | source)
XLA Modules:
  0.0 199.6 jit_solution(14026242389526518541)
XLA Ops:
  0.6 9.0 %pack_soundings.1.blocks_hbm = f32[128,40,128]{2,1,0:T(8,128)} custom-call(f32[72,2048]{1,0:T(8,128)} %blocks_ref.1, s32[16,128]{1,0:T(8,128)} %bitcast.6, s32[16,128]{1,0:T(8,128)} %bitcast.7), custom_call_target="tpu_custom_call" | custom-call | tf_op jit(solution)/shard_map/pack_soundings/pallas_call | solution.py:92
  9.6 76.9 %first_step.1 = (f32[72,2,64,128]{3,2,1,0:T(8,128)}, f32[128,40,128]{2,1,0:T(8,128)}) custom-call(f32[72,2,64,128]{3,2,1,0:T(8,128)} %a_hbm.1, f32[2,72,64,128]{3,2,1,0:T(8,128)} %face_ref.1, f32[71,64,128]{2,1,0:T(8,128)} %m_hbm.3, f32[128,40,128]{2,1,0:T(8,128)} %pack_soundings.1.blocks_hbm), custom_call_target="tpu_custom_call" | custom-call | tf_op jit(solution)/shard_map/first_step/pallas_call | solution.py:423
  86.6 30.8 %add_forcing.1 = f32[72,128,128]{2,1,0:T(8,128)} custom-call(f32[128,40,128]{2,1,0:T(8,128)} %get-tuple-element.6.got_ref, f32[9216,128]{1,0:T(8,128)} %bitcast.4), custom_call_target="tpu_custom_call" | custom-call | tf_op jit(solution)/shard_map/add_forcing/pallas_call | solution.py:585
  117.4 21.6 %second_front.1 = (f32[72,2,64,128]{3,2,1,0:T(8,128)}, f32[2,2,64,128]{3,2,1,0:T(8,128)}) custom-call(f32[72,2,64,128]{3,2,1,0:T(8,128)} %bitcast.5, f32[2,72,64,128]{3,2,1,0:T(8,128)} %face_ref.1, f32[71,64,128]{2,1,0:T(8,128)} %m_hbm.3), custom_call_target="tpu_custom_call" | custom-call | tf_op jit(solution)/shard_map/second_front/pallas_call | solution.py:448
  139.0 60.6 %last_sweep.1 = (f32[72,2,64,128]{3,2,1,0:T(8,128)}, f32[2,64,128]{2,1,0:T(8,128)}) custom-call(f32[72,2,64,128]{3,2,1,0:T(8,128)} %get-tuple-element.8.cells_ref, f32[2,72,64,128]{3,2,1,0:T(8,128)} %face_ref.1, f32[2,2,64,128]{3,2,1,0:T(8,128)} %get-tuple-element.9.sides_ref, f32[72,2,64,128]{3,2,1,0:T(8,128)} %get-tuple-element.7.ground_ref), custom_call_target="tpu_custom_call" | custom-call | tf_op jit(solution)/shard_map/last_sweep/pallas_call | solution.py:482

commit v2 on v1

--- a/solution.py
+++ b/solution.py
@@ -297,7 +297,7 @@
 FRONT = 18
 
 
-def sweep_columns(levels, tracers, lane, load_face, load_cells, load_sides, store):
+def sweep_columns(levels, tracers, lane, load_face, load_cells, store):
     tile = lane.shape[1]
     for k in range(levels):
         face = load_face(k)
@@ -306,14 +306,28 @@
             cells = load_cells(k, t)
             rise = jnp.where(lane == tile - 1, 0.0, pltpu.roll(cells, tile - 1, 1) - cells)
             swept = cells + out_face * rise + pltpu.roll(in_face * rise, 1, 1)
-            if load_sides is not None:
-                swept = swept + sides_of(lane, load_sides(k, t), k)
             store(k, t, swept)
 
 
-def sides_of(lane, merged, k):
+def add_sides(levels, tracers, lane, obuf, merged, span):
     tile = lane.shape[1]
-    return jnp.where((lane == 0) | (lane == tile - 1), pltpu.roll(merged, tile - 1 - k, 1), 0.0)
+    ends = (lane == 0) | (lane == tile - 1)
+    for t in range(tracers):
+        sides = [merged[t, 0, span, :], merged[t, 1, span, :]]
+        for k in range(levels):
+            turned = pltpu.roll(sides[k % 2], tile - 1 - k, 1)
+            obuf[k, t, span, :] = obuf[k, t, span, :] + jnp.where(ends, turned, 0.0)
+
+
+def peer_at(step, lon_count, lat_count):
+    shift = lax.rem(step * 53, lon_count * lat_count)
+    lon, lat = lax.axis_index("lon"), lax.axis_index("lat")
+    wide = lon_count // 8
+    x = lax.rem(lon // 8 + shift // 32, wide)
+    y = lax.rem(lax.rem(lon // 2, 4) + lax.rem(shift // 8, 4), 4)
+    z = lax.rem((lat // 2) * 2 + lax.rem(lon, 2) + lax.rem(shift // 2, 4), 4)
+    core = lax.rem(lat + shift, 2)
+    return x * 8 + y * 2 + lax.rem(z, 2), (z // 2) * 2 + core
 
 
 def first_kernel(lon_count, lat_count, a_hbm, c_hbm, m_hbm, blocks_hbm, out_hbm, got_hbm, *scratch):
@@ -326,12 +340,11 @@
     def trade(begin, end):
         @pl.loop(begin, end)
         def _(i):
-            peer = lax.rem(me + i, devices)
+            lon, lat = peer_at(i, lon_count, lat_count)
             pltpu.make_async_remote_copy(
-                src_ref=blocks_hbm.at[peer], dst_ref=got_hbm.at[me],
+                src_ref=blocks_hbm.at[lon * lat_count + lat], dst_ref=got_hbm.at[me],
                 send_sem=trade_send, recv_sem=trade_recv,
-                device_id={"lon": peer // lat_count, "lat": lax.rem(peer, lat_count)},
-                device_id_type=MESH,
+                device_id={"lon": lon, "lat": lat}, device_id_type=MESH,
             ).start()
 
     cuts = (1, 1 + devices // 4, devices // 2, devices)
@@ -363,24 +376,21 @@
 
             sweep_columns(
                 levels, tracers, lane, lambda k: c_ref[0, k, span, :],
-                lambda k, t: vbuf[k, t, span, :], None, store,
+                lambda k, t: vbuf[k, t, span, :], store,
             )
 
     hooks = (at_entry, lambda: trade(cuts[1], cuts[2]), lambda: trade(cuts[2], cuts[3]), main_sweep)
     transport_front(lon_count, lat_count, hooks, a_hbm, c_hbm, m_hbm, front)
 
-    def stored(g):
-        span = pl.ds(pl.multiple_of(g * 8, 8), 8)
-        return pltpu.make_async_copy(obuf.at[:, :, span, :], out_hbm.at[:, :, span, :], store_sem.at[g])
+    def stored(t, r):
+        return pltpu.make_async_copy(obuf.at[:, t, r, :], out_hbm.at[t, r], store_sem.at[t * band + r])
 
     @pl.loop(0, band // 8)
     def _(g):
-        span = pl.ds(pl.multiple_of(g * 8, 8), 8)
+        add_sides(levels, tracers, lane, obuf, merged, pl.ds(pl.multiple_of(g * 8, 8), 8))
         for t in range(tracers):
-            sides = [merged[t, 0, span, :], merged[t, 1, span, :]]
-            for k in range(levels):
-                obuf[k, t, span, :] = obuf[k, t, span, :] + sides_of(lane, sides[k % 2], k)
-        stored(g).start()
+            for r in range(8):
+                stored(t, g * 8 + r).start()
 
     pltpu.make_async_copy(blocks_hbm.at[me], got_hbm.at[me], own_sem).wait()
     most = pl.ds(0, devices - 1)
@@ -391,9 +401,10 @@
         device_id_type=MESH,
     ).wait()
 
-    @pl.loop(0, band // 8)
-    def _(g):
-        stored(g).wait()
+    @pl.loop(0, band)
+    def _(r):
+        for t in range(tracers):
+            stored(t, r).wait()
 
 
 def second_kernel(lon_count, lat_count, a_hbm, c_hbm, m_hbm, out_hbm, sides_ref, *scratch):
@@ -423,7 +434,7 @@
     return pl.pallas_call(
         functools.partial(first_kernel, lon_count, lat_count),
         out_shape=(
-            jax.ShapeDtypeStruct(state.shape, jnp.float32),
+            jax.ShapeDtypeStruct((tracers, band, levels, tile), jnp.float32),
             jax.ShapeDtypeStruct(blocks.shape, jnp.float32),
         ),
         in_specs=[ANY] * 4,
@@ -431,7 +442,7 @@
         scratch_shapes=front_scratch(levels, tracers, band, tile)
         + [
             pltpu.VMEM((levels, tracers, band, tile), jnp.float32),
-            pltpu.SemaphoreType.DMA((band // 8,)),
+            pltpu.SemaphoreType.DMA((tracers * band,)),
             pltpu.SemaphoreType.DMA,
             pltpu.SemaphoreType.DMA,
             pltpu.SemaphoreType.DMA,
@@ -461,41 +472,85 @@
     )(state, courant, mixing)
 
 
-def last_kernel(cells_ref, face_ref, sides_ref, ground_ref, out_ref, flux_ref):
-    levels, tracers, _, tile = cells_ref.shape
+def last_kernel(
+    cells_hbm, c_hbm, sides_ref, first_hbm, out_hbm, flux_ref, cells, faces, obuf, ground, cell_sem, face_sem,
+    store_sem, ground_sem,
+):
+    levels, tracers, band, tile = cells.shape
     lane = lane_iota((8, tile))
-    sides = [[sides_ref[t, p] for p in range(2)] for t in range(tracers)]
-
-    def store(k, t, swept):
-        out_ref[k, t] = swept
-        if k == 0:
-            flux_ref[t] = ground_ref[0, t] + swept
-
-    sweep_columns(
-        levels, tracers, lane, lambda k: face_ref[0, k], lambda k, t: cells_ref[k, t],
-        lambda k, t: sides[t][k % 2], store,
-    )
+
+    def rows_of(g):
+        return pl.ds(pl.multiple_of(g * 8, 8), 8)
+
+    def load_cells(g):
+        return pltpu.make_async_copy(
+            cells_hbm.at[:, :, rows_of(g), :], cells.at[:, :, rows_of(g), :], cell_sem.at[g]
+        )
+
+    def load_faces(g):
+        return pltpu.make_async_copy(
+            c_hbm.at[0, :, rows_of(g), :], faces.at[:, rows_of(g), :], face_sem.at[g]
+        )
+
+    def stored(g):
+        return pltpu.make_async_copy(
+            obuf.at[:, :, rows_of(g), :], out_hbm.at[:, :, rows_of(g), :], store_sem.at[g]
+        )
+
+    @pl.loop(0, band // 8)
+    def _(g):
+        load_cells(g).start()
+        load_faces(g).start()
+
+    load_ground = pltpu.make_async_copy(first_hbm.at[:, :, 0, :], ground, ground_sem)
+    load_ground.start()
+
+    @pl.loop(0, band // 8)
+    def _(g):
+        load_cells(g).wait()
+        load_faces(g).wait()
+        span = rows_of(g)
+
+        def store(k, t, swept):
+            obuf[k, t, span, :] = swept
+
+        sweep_columns(
+            levels, tracers, lane, lambda k: faces[k, span, :], lambda k, t: cells[k, t, span, :], store
+        )
+
+    @pl.loop(0, band // 8)
+    def _(g):
+        add_sides(levels, tracers, lane, obuf, sides_ref, rows_of(g))
+        stored(g).start()
+
+    load_ground.wait()
+    flux_ref[...] = ground[...] + obuf[0]
+
+    @pl.loop(0, band // 8)
+    def _(g):
+        stored(g).wait()
 
 
 def last_sweep(cells, courant, sides, after_first):
     levels, tracers, band, tile = cells.shape
     return pl.pallas_call(
         last_kernel,
-        grid=(band // 8,),
         out_shape=(
             jax.ShapeDtypeStruct(cells.shape, jnp.float32),
             jax.ShapeDtypeStruct(cells.shape[1:], jnp.float32),
         ),
-        in_specs=[
-            pl.BlockSpec((levels, tracers, 8, tile), lambda g: (0, 0, g, 0)),
-            pl.BlockSpec((1, levels, 8, tile), lambda g: (0, 0, g, 0)),
-            pl.BlockSpec((tracers, 2, 8, tile), lambda g: (0, 0, g, 0)),
-            pl.BlockSpec((1, tracers, 8, tile), lambda g: (0, 0, g, 0)),
+        in_specs=[ANY, ANY, pl.BlockSpec(memory_space=pltpu.VMEM), ANY],
+        out_specs=(ANY, pl.BlockSpec(memory_space=pltpu.VMEM)),
+        scratch_shapes=[
+            pltpu.VMEM((levels, tracers, band, tile), jnp.float32),
+            pltpu.VMEM((levels, band, tile), jnp.float32),
+            pltpu.VMEM((levels, tracers, band, tile), jnp.float32),
+            pltpu.VMEM((tracers, band, tile), jnp.float32),
+            pltpu.SemaphoreType.DMA((band // 8,)),
+            pltpu.SemaphoreType.DMA((band // 8,)),
+            pltpu.SemaphoreType.DMA((band // 8,)),
+            pltpu.SemaphoreType.DMA,
         ],
-        out_specs=(
-            pl.BlockSpec((levels, tracers, 8, tile), lambda g: (0, 0, g, 0)),
-            pl.BlockSpec((tracers, 8, tile), lambda g: (0, g, 0)),
-        ),
         compiler_params=pltpu.CompilerParams(vmem_limit_bytes=VMEM_LIMIT),
         name="last_sweep",
     )(cells, courant, sides, after_first)
@@ -542,10 +597,10 @@
     def _(pair):
         to_smem(pair).wait()
 
-    @pl.loop(0, devices * capacity // (4 * STREAMS))
+    @pl.loop(0, devices * capacity // (8 * STREAMS))
     def _(part):
-        for i in range(4):
-            at = [part * 4 * STREAMS + i * STREAMS + s for s in range(STREAMS)]
+        for i in range(8):
+            at = [part * 8 * STREAMS + i * STREAMS + s for s in range(STREAMS)]
             cell = [ids_smem[at[s]] for s in range(STREAMS)]
             new = [sums[s][pl.ds(cell[s], 1), :] + rows[pl.ds(at[s], 1), :] for s in range(STREAMS)]
             for s in range(STREAMS):
@@ -553,11 +608,11 @@
 
     load.wait()
 
-    def stored(part):
-        span = pl.ds(pl.multiple_of(part * group, group), group)
-        return pltpu.make_async_copy(
-            total.reshape(levels, lines, LANES).at[:, span, :], out_hbm.at[:, span, :], store_sem.at[part]
-        )
+    def level_rows(line):
+        return pl.ds(pl.multiple_of(line * levels, 8), levels)
+
+    def stored(line):
+        return pltpu.make_async_copy(total.at[level_rows(line)], out_hbm.at[:, line, :], store_sem.at[line])
 
     @pl.loop(0, lines // group)
     def _(part):
@@ -569,17 +624,18 @@
                 total_here = total_here + sums[s][span, :]
             turned.append(total_here.T[:levels])
         for i in range(group):
-            at = pl.ds(part * group + i, levels, stride=lines)
+            at = level_rows(part * group + i)
             total[at, :] = state[at, :] + turned[i]
-        stored(part).start()
-
-    @pl.loop(0, lines // group)
-    def _(part):
-        stored(part).wait()
+        for i in range(group):
+            stored(part * group + i).start()
+
+    @pl.loop(0, lines)
+    def _(line):
+        stored(line).wait()
 
 
 def add_forcing(got, after_first, capacity):
-    levels, tracers, band, tile = after_first.shape
+    tracers, band, levels, tile = after_first.shape
     devices = got.shape[0]
     lines = tracers * band
     out = pl.pallas_call(
@@ -598,12 +654,12 @@
         + [
             pltpu.SemaphoreType.DMA((devices // 2,)),
             pltpu.SemaphoreType.DMA,
-            pltpu.SemaphoreType.DMA((lines // 8,)),
+            pltpu.SemaphoreType.DMA((lines,)),
         ],
         compiler_params=pltpu.CompilerParams(vmem_limit_bytes=VMEM_LIMIT),
         name="add_forcing",
     )(got, after_first.reshape(levels * lines, tile))
-    return out.reshape(after_first.shape)
+    return out.reshape(levels, tracers, band, tile)
 
 
 def on_device(adjoint_in, courant, mixing, kernel_blocks, sounding_dest, sounding_cell):

time: 200 us -> 120 us (0.60)
  the two profiles are of different devices: /device:TPU:6 before, /device:TPU:1 now
where the time goes in v2:
time: 120 us
  Pallas kernels  119 us (99%)
    pallas_call x1, Pallas kernels, first_step(): pl.pallas_call(functools.partial(first_kernel, lon_count, lat_count), out...  55 us
    pallas_call x1, Pallas kernels, add_forcing(): pl.pallas_call(functools.partial(force_kernel, capacity, levels, lines),...  28.8 us
    pallas_call x1, Pallas kernels, second_front(): pl.pallas_call(functools.partial(second_kernel, lon_count, lat_count), ou...  17 us
    pallas_call x1, Pallas kernels, last_sweep(): pl.pallas_call(last_kernel, out_shape=(jax.ShapeDtypeStruct(cells.shape,...  9.38 us
    pallas_call x1, Pallas kernels, pack(): pl.pallas_call(functools.partial(pack_kernel, devices, capacity, levels),...  9 us

profile of v2, /device:TPU:1, one launch (start us, length us, event | category | flops | bytes accessed | tf_op | source)
XLA Modules:
  0.0 119.8 jit_solution(11172744657993751861)
XLA Ops:
  0.6 9.0 %pack_soundings.1.blocks_hbm = f32[128,40,128]{2,1,0:T(8,128)} custom-call(f32[72,2048]{1,0:T(8,128)} %blocks_ref.1, s32[16,128]{1,0:T(8,128)} %bitcast.6, s32[16,128]{1,0:T(8,128)} %bitcast.7), custom_call_target="tpu_custom_call" | custom-call | tf_op jit(solution)/shard_map/pack_soundings/pallas_call | solution.py:92
  9.6 55.0 %first_step.1 = (f32[2,64,72,128]{3,2,1,0:T(8,128)}, f32[128,40,128]{2,1,0:T(8,128)}) custom-call(f32[72,2,64,128]{3,2,1,0:T(8,128)} %a_hbm.1, f32[2,72,64,128]{3,2,1,0:T(8,128)} %c_hbm.5, f32[71,64,128]{2,1,0:T(8,128)} %m_hbm.3, f32[128,40,128]{2,1,0:T(8,128)} %pack_soundings.1.blocks_hbm), custom_call_target="tpu_custom_call" | custom-call | tf_op jit(solution)/shard_map/first_step/pallas_call | solution.py:434
  64.7 28.8 %add_forcing.1 = f32[72,128,128]{2,1,0:T(8,128)} custom-call(f32[128,40,128]{2,1,0:T(8,128)} %get-tuple-element.6.got_ref, f32[9216,128]{1,0:T(8,128)} %bitcast.4), custom_call_target="tpu_custom_call" | custom-call | tf_op jit(solution)/shard_map/add_forcing/pallas_call | solution.py:641
  93.4 17.0 %second_front.1 = (f32[72,2,64,128]{3,2,1,0:T(8,128)}, f32[2,2,64,128]{3,2,1,0:T(8,128)}) custom-call(f32[72,2,64,128]{3,2,1,0:T(8,128)} %bitcast.5, f32[2,72,64,128]{3,2,1,0:T(8,128)} %c_hbm.5, f32[71,64,128]{2,1,0:T(8,128)} %m_hbm.3), custom_call_target="tpu_custom_call" | custom-call | tf_op jit(solution)/shard_map/second_front/pallas_call | solution.py:459
  110.5 9.4 %last_sweep.1 = (f32[72,2,64,128]{3,2,1,0:T(8,128)}, f32[2,64,128]{2,1,0:T(8,128)}) custom-call(f32[72,2,64,128]{3,2,1,0:T(8,128)} %get-tuple-element.8.cells_hbm, f32[2,72,64,128]{3,2,1,0:T(8,128)} %c_hbm.5, f32[2,2,64,128]{3,2,1,0:T(8,128)} %get-tuple-element.9.sides_ref, f32[2,64,72,128]{3,2,1,0:T(8,128)} %get-tuple-element.7.first_hbm), custom_call_target="tpu_custom_call" | custom-call | tf_op jit(solution)/shard_map/last_sweep/pallas_call | solution.py:536

commit v3 on v2

--- a/solution.py
+++ b/solution.py
@@ -9,8 +9,10 @@
 MESH = pl.DeviceIdType.MESH
 ANY = pl.BlockSpec(memory_space=pl.ANY)
 LANES = 128
-HALF = 40
+HALF = 37
+ROOM = 40
 STREAMS = 4
+CHUNKS = 4
 VMEM_LIMIT = 60 * 1024 * 1024
 
 
@@ -83,15 +85,15 @@
         for i, wide in enumerate(wides):
             first, second = wide[:HALF], wide[HALF : 2 * HALF]
             pair = part * group + i
-            out_ref[2 * pair] = jnp.where(low, first, pltpu.roll(second, capacity, 1))
-            out_ref[2 * pair + 1] = jnp.where(low, pltpu.roll(first, capacity, 1), second)
+            out_ref[2 * pair, :HALF] = jnp.where(low, first, pltpu.roll(second, capacity, 1))
+            out_ref[2 * pair + 1, :HALF] = jnp.where(low, pltpu.roll(first, capacity, 1), second)
 
 
 def pack(kernel_blocks, owner, cell, devices, capacity):
     levels, held = kernel_blocks.shape
     return pl.pallas_call(
         functools.partial(pack_kernel, devices, capacity, levels),
-        out_shape=jax.ShapeDtypeStruct((devices, HALF, LANES), jnp.float32),
+        out_shape=jax.ShapeDtypeStruct((devices, ROOM, LANES), jnp.float32),
         in_specs=[pl.BlockSpec(memory_space=pltpu.VMEM)] * 3,
         out_specs=pl.BlockSpec(memory_space=pltpu.VMEM),
         scratch_shapes=[
@@ -111,7 +113,7 @@
         a_ref, c_ref, m_ref, vbuf, rbuf, send_n, send_s, send_e, send_w,
         from_s, from_n, from_w, from_e, rows_fix, merged, load_sem, send_sem, recv_sem,
     ) = front
-    at_entry, after_rows, after_columns, during_columns = hooks
+    at_entry, before_rows, after_rows, after_columns, during_columns = hooks
     levels, tracers, band, tile = a_ref.shape
     lon, lat = lax.axis_index("lon"), lax.axis_index("lat")
     north = {"lon": lon, "lat": lax.rem(lat + 1, lat_count)}
@@ -119,11 +121,13 @@
     east = {"lon": lax.rem(lon + 1, lon_count), "lat": lat}
     west = {"lon": lax.rem(lon + lon_count - 1, lon_count), "lat": lat}
 
-    loads = [
-        pltpu.make_async_copy(m_hbm, m_ref, load_sem.at[0]),
-        pltpu.make_async_copy(a_hbm, a_ref, load_sem.at[1]),
-        pltpu.make_async_copy(c_hbm, c_ref, load_sem.at[2]),
-    ]
+    cuts = [levels * i // CHUNKS for i in range(CHUNKS)] + [levels]
+    loads = []
+    for i in range(CHUNKS):
+        span, faces = slice(cuts[i], cuts[i + 1]), slice(cuts[i], min(cuts[i + 1], levels - 1))
+        loads.append(pltpu.make_async_copy(m_hbm.at[faces], m_ref.at[faces], load_sem.at[2 * i]))
+        loads.append(pltpu.make_async_copy(a_hbm.at[span], a_ref.at[span], load_sem.at[2 * i + 1]))
+    loads.append(pltpu.make_async_copy(c_hbm, c_ref, load_sem.at[2 * CHUNKS]))
     for load in loads:
         load.start()
     at_entry()
@@ -147,7 +151,13 @@
         vbuf[k] = solved
         return mix, ratio, solved
 
-    mix, ratio, solved = lax.fori_loop(1, levels - 1, down, (mix, ratio, solved))
+    carry = (mix, ratio, solved)
+    for i in range(CHUNKS):
+        if i > 0:
+            loads[2 * i].wait()
+            loads[2 * i + 1].wait()
+        carry = lax.fori_loop(max(cuts[i], 1), min(cuts[i + 1], levels - 1), down, carry)
+    mix, ratio, solved = carry
     inverse = 1.0 / (1.0 + mix - mix * ratio)
     solved = (a_ref[levels - 1] + mix[None] * solved) * inverse[None]
 
@@ -167,7 +177,7 @@
 
     lax.fori_loop(0, levels - 1, up, solved)
 
-    loads[2].wait()
+    loads[2 * CHUNKS].wait()
     edge = jnp.where(lat == lat_count - 1, 0.0, 1.0)
 
     @pl.loop(0, levels // 8)
@@ -184,6 +194,7 @@
 
     to_north = remote(0, send_n, from_s, north)
     to_south = remote(1, send_s, from_n, south)
+    before_rows()
     to_north.start()
     to_south.start()
     after_rows()
@@ -288,7 +299,7 @@
         pltpu.VMEM((tracers, band, tile), f32),
         pltpu.VMEM((2 * tracers * levels, tile), f32),
         pltpu.VMEM((tracers, 2, band, tile), f32),
-        pltpu.SemaphoreType.DMA((3,)),
+        pltpu.SemaphoreType.DMA((2 * CHUNKS + 1,)),
         pltpu.SemaphoreType.DMA((4,)),
         pltpu.SemaphoreType.DMA((4,)),
     ]
@@ -297,26 +308,32 @@
 FRONT = 18
 
 
-def sweep_columns(levels, tracers, lane, load_face, load_cells, store):
-    tile = lane.shape[1]
-    for k in range(levels):
-        face = load_face(k)
-        out_face, in_face = jnp.maximum(face, 0.0), jnp.minimum(face, 0.0)
-        for t in range(tracers):
-            cells = load_cells(k, t)
-            rise = jnp.where(lane == tile - 1, 0.0, pltpu.roll(cells, tile - 1, 1) - cells)
-            swept = cells + out_face * rise + pltpu.roll(in_face * rise, 1, 1)
-            store(k, t, swept)
-
-
-def add_sides(levels, tracers, lane, obuf, merged, span):
-    tile = lane.shape[1]
+def sweep_all(c_ref, vbuf, obuf, done):
+    levels, tracers, band, tile = vbuf.shape
+    lane = lane_iota((8, tile))
+
+    @pl.loop(0, band // 8)
+    def _(g):
+        span = pl.ds(pl.multiple_of(g * 8, 8), 8)
+        for k in range(levels):
+            face = c_ref[0, k, span, :]
+            out_face, in_face = jnp.maximum(face, 0.0), jnp.minimum(face, 0.0)
+            for t in range(tracers):
+                cells = vbuf[k, t, span, :]
+                rise = jnp.where(lane == tile - 1, 0.0, pltpu.roll(cells, tile - 1, 1) - cells)
+                obuf[k, t, span, :] = cells + out_face * rise + pltpu.roll(in_face * rise, 1, 1)
+        done(g)
+
+
+def add_sides(cells, merged, span, out):
+    levels, tracers, band, tile = cells.shape
+    lane = lane_iota((8, tile))
     ends = (lane == 0) | (lane == tile - 1)
     for t in range(tracers):
         sides = [merged[t, 0, span, :], merged[t, 1, span, :]]
         for k in range(levels):
             turned = pltpu.roll(sides[k % 2], tile - 1 - k, 1)
-            obuf[k, t, span, :] = obuf[k, t, span, :] + jnp.where(ends, turned, 0.0)
+            out[k, t, span, :] = cells[k, t, span, :] + jnp.where(ends, turned, 0.0)
 
 
 def peer_at(step, lon_count, lat_count):
@@ -336,18 +353,19 @@
     levels, tracers, band, tile = vbuf.shape
     devices = lon_count * lat_count
     me = lax.axis_index("lon") * lat_count + lax.axis_index("lat")
+    used = pl.ds(0, HALF)
 
     def trade(begin, end):
         @pl.loop(begin, end)
         def _(i):
             lon, lat = peer_at(i, lon_count, lat_count)
             pltpu.make_async_remote_copy(
-                src_ref=blocks_hbm.at[lon * lat_count + lat], dst_ref=got_hbm.at[me],
+                src_ref=blocks_hbm.at[lon * lat_count + lat, used], dst_ref=got_hbm.at[me, used],
                 send_sem=trade_send, recv_sem=trade_recv,
                 device_id={"lon": lon, "lat": lat}, device_id_type=MESH,
             ).start()
 
-    cuts = (1, 1 + devices // 4, devices // 2, devices)
+    early = 1 + devices // 5
 
     def at_entry():
         barrier = pltpu.get_barrier_semaphore()
@@ -360,26 +378,15 @@
                 device_id_type=MESH,
             )
 
-        pl.semaphore_wait(barrier, devices - 1)
-        trade(cuts[0], cuts[1])
         pltpu.make_async_copy(blocks_hbm.at[me], got_hbm.at[me], own_sem).start()
 
-    lane = lane_iota((8, tile))
+    def before_rows():
+        pl.semaphore_wait(pltpu.get_barrier_semaphore(), devices - 1)
 
     def main_sweep():
-        @pl.loop(0, band // 8)
-        def _(g):
-            span = pl.ds(pl.multiple_of(g * 8, 8), 8)
-
-            def store(k, t, swept):
-                obuf[k, t, span, :] = swept
-
-            sweep_columns(
-                levels, tracers, lane, lambda k: c_ref[0, k, span, :],
-                lambda k, t: vbuf[k, t, span, :], store,
-            )
-
-    hooks = (at_entry, lambda: trade(cuts[1], cuts[2]), lambda: trade(cuts[2], cuts[3]), main_sweep)
+        sweep_all(c_ref, vbuf, obuf, lambda g: None)
+
+    hooks = (at_entry, before_rows, lambda: trade(1, early), lambda: trade(early, devices), main_sweep)
     transport_front(lon_count, lat_count, hooks, a_hbm, c_hbm, m_hbm, front)
 
     def stored(t, r):
@@ -387,7 +394,7 @@
 
     @pl.loop(0, band // 8)
     def _(g):
-        add_sides(levels, tracers, lane, obuf, merged, pl.ds(pl.multiple_of(g * 8, 8), 8))
+        add_sides(obuf, merged, pl.ds(pl.multiple_of(g * 8, 8), 8), obuf)
         for t in range(tracers):
             for r in range(8):
                 stored(t, g * 8 + r).start()
@@ -395,7 +402,7 @@
     pltpu.make_async_copy(blocks_hbm.at[me], got_hbm.at[me], own_sem).wait()
     most = pl.ds(0, devices - 1)
     pltpu.make_async_remote_copy(
-        src_ref=blocks_hbm.at[most], dst_ref=got_hbm.at[most],
+        src_ref=blocks_hbm.at[most, used], dst_ref=got_hbm.at[most, used],
         send_sem=trade_send, recv_sem=trade_recv,
         device_id={"lon": lax.axis_index("lon"), "lat": lax.rem(lax.axis_index("lat") + 1, lat_count)},
         device_id_type=MESH,
@@ -408,8 +415,9 @@
 
 
 def second_kernel(lon_count, lat_count, a_hbm, c_hbm, m_hbm, out_hbm, sides_ref, *scratch):
-    front, (store_sem,) = scratch[:FRONT], scratch[FRONT:]
-    vbuf, merged = front[3], front[14]
+    front, (obuf, store_sem) = scratch[:FRONT], scratch[FRONT:]
+    c_ref, vbuf, merged = front[1], front[3], front[14]
+    band = vbuf.shape[2]
 
     def at_entry():
         lon, lat = lax.axis_index("lon"), lax.axis_index("lat")
@@ -420,13 +428,24 @@
                 device_id={"lon": lax.rem(lon + d_lon, lon_count), "lat": lax.rem(lat + d_lat, lat_count)},
                 device_id_type=MESH,
             )
-        pl.semaphore_wait(barrier, 4)
-
-    store = pltpu.make_async_copy(vbuf, out_hbm, store_sem)
-    hooks = (at_entry, lambda: None, store.start, lambda: None)
+
+    def before_rows():
+        pl.semaphore_wait(pltpu.get_barrier_semaphore(), 4)
+
+    def stored(g):
+        span = pl.ds(pl.multiple_of(g * 8, 8), 8)
+        return pltpu.make_async_copy(obuf.at[:, :, span, :], out_hbm.at[:, :, span, :], store_sem.at[g])
+
+    def main_sweep():
+        sweep_all(c_ref, vbuf, obuf, lambda g: stored(g).start())
+
+    hooks = (at_entry, before_rows, lambda: None, lambda: None, main_sweep)
     transport_front(lon_count, lat_count, hooks, a_hbm, c_hbm, m_hbm, front)
     sides_ref[...] = merged[...]
-    store.wait()
+
+    @pl.loop(0, band // 8)
+    def _(g):
+        stored(g).wait()
 
 
 def first_step(state, courant, mixing, blocks, lon_count, lat_count):
@@ -464,7 +483,8 @@
         ),
         in_specs=[ANY] * 3,
         out_specs=(ANY, pl.BlockSpec(memory_space=pltpu.VMEM)),
-        scratch_shapes=front_scratch(levels, tracers, band, tile) + [pltpu.SemaphoreType.DMA],
+        scratch_shapes=front_scratch(levels, tracers, band, tile)
+        + [pltpu.VMEM((levels, tracers, band, tile), jnp.float32), pltpu.SemaphoreType.DMA((band // 8,))],
         compiler_params=pltpu.CompilerParams(
             collective_id=1, has_side_effects=True, vmem_limit_bytes=VMEM_LIMIT
         ),
@@ -473,23 +493,16 @@
 
 
 def last_kernel(
-    cells_hbm, c_hbm, sides_ref, first_hbm, out_hbm, flux_ref, cells, faces, obuf, ground, cell_sem, face_sem,
-    store_sem, ground_sem,
+    cells_hbm, sides_ref, first_hbm, out_hbm, flux_ref, cells, obuf, ground, cell_sem, store_sem, ground_sem
 ):
-    levels, tracers, band, tile = cells.shape
-    lane = lane_iota((8, tile))
+    band = cells.shape[2]
 
     def rows_of(g):
         return pl.ds(pl.multiple_of(g * 8, 8), 8)
 
-    def load_cells(g):
+    def load(g):
         return pltpu.make_async_copy(
             cells_hbm.at[:, :, rows_of(g), :], cells.at[:, :, rows_of(g), :], cell_sem.at[g]
-        )
-
-    def load_faces(g):
-        return pltpu.make_async_copy(
-            c_hbm.at[0, :, rows_of(g), :], faces.at[:, rows_of(g), :], face_sem.at[g]
         )
 
     def stored(g):
@@ -499,28 +512,15 @@
 
     @pl.loop(0, band // 8)
     def _(g):
-        load_cells(g).start()
-        load_faces(g).start()
+        load(g).start()
 
     load_ground = pltpu.make_async_copy(first_hbm.at[:, :, 0, :], ground, ground_sem)
     load_ground.start()
 
     @pl.loop(0, band // 8)
     def _(g):
-        load_cells(g).wait()
-        load_faces(g).wait()
-        span = rows_of(g)
-
-        def store(k, t, swept):
-            obuf[k, t, span, :] = swept
-
-        sweep_columns(
-            levels, tracers, lane, lambda k: faces[k, span, :], lambda k, t: cells[k, t, span, :], store
-        )
-
-    @pl.loop(0, band // 8)
-    def _(g):
-        add_sides(levels, tracers, lane, obuf, sides_ref, rows_of(g))
+        load(g).wait()
+        add_sides(cells, sides_ref, rows_of(g), obuf)
         stored(g).start()
 
     load_ground.wait()
@@ -531,7 +531,7 @@
         stored(g).wait()
 
 
-def last_sweep(cells, courant, sides, after_first):
+def last_part(cells, sides, after_first):
     levels, tracers, band, tile = cells.shape
     return pl.pallas_call(
         last_kernel,
@@ -539,31 +539,39 @@
             jax.ShapeDtypeStruct(cells.shape, jnp.float32),
             jax.ShapeDtypeStruct(cells.shape[1:], jnp.float32),
         ),
-        in_specs=[ANY, ANY, pl.BlockSpec(memory_space=pltpu.VMEM), ANY],
+        in_specs=[ANY, pl.BlockSpec(memory_space=pltpu.VMEM), ANY],
         out_specs=(ANY, pl.BlockSpec(memory_space=pltpu.VMEM)),
         scratch_shapes=[
             pltpu.VMEM((levels, tracers, band, tile), jnp.float32),
-            pltpu.VMEM((levels, band, tile), jnp.float32),
             pltpu.VMEM((levels, tracers, band, tile), jnp.float32),
             pltpu.VMEM((tracers, band, tile), jnp.float32),
-            pltpu.SemaphoreType.DMA((band // 8,)),
             pltpu.SemaphoreType.DMA((band // 8,)),
             pltpu.SemaphoreType.DMA((band // 8,)),
             pltpu.SemaphoreType.DMA,
         ],
         compiler_params=pltpu.CompilerParams(vmem_limit_bytes=VMEM_LIMIT),
-        name="last_sweep",
-    )(cells, courant, sides, after_first)
-
-
-def force_kernel(capacity, levels, lines, got_ref, state_hbm, out_hbm, rows, ids, ids_smem, state, total, *rest):
-    sums, (ids_sem, load_sem, store_sem) = rest[:STREAMS], rest[STREAMS:]
+        name="last_part",
+    )(cells, sides, after_first)
+
+
+def force_kernel(capacity, levels, lines, got_hbm, state_hbm, out_hbm, got_ref, rows, ids, ids_smem, state, total, *rest):
+    sums, (got_sem, ids_sem, load_sem, store_sem) = rest[:STREAMS], rest[STREAMS:]
     devices = got_ref.shape[0]
     cells_all = lines * LANES
+    load_got = pltpu.make_async_copy(got_hbm, got_ref, got_sem)
+    load_got.start()
     load = pltpu.make_async_copy(state_hbm, state, load_sem)
     load.start()
     low = lane_iota((HALF, LANES)) < capacity
     group = 8
+    zero = jnp.zeros((64, LANES), jnp.float32)
+
+    @pl.loop(0, cells_all // 64)
+    def _(i):
+        for s in range(STREAMS):
+            sums[s][pl.ds(pl.multiple_of(i * 64, 64), 64), :] = zero
+
+    load_got.wait()
 
     def to_smem(pair):
         return pltpu.make_async_copy(
@@ -574,7 +582,7 @@
     def _(part):
         for i in range(group):
             pair = part * group + i
-            one, two = got_ref[2 * pair], got_ref[2 * pair + 1]
+            one, two = got_ref[2 * pair, :HALF], got_ref[2 * pair + 1, :HALF]
             first = jnp.where(low, one, pltpu.roll(two, capacity, 1))
             second = jnp.where(low, pltpu.roll(one, capacity, 1), two)
             cell = second[levels - HALF : levels - HALF + 1, :].astype(jnp.int32)
@@ -585,13 +593,6 @@
     @pl.loop(0, devices // 2)
     def _(pair):
         to_smem(pair).start()
-
-    zero = jnp.zeros((64, LANES), jnp.float32)
-
-    @pl.loop(0, cells_all // 64)
-    def _(i):
-        for s in range(STREAMS):
-            sums[s][pl.ds(pl.multiple_of(i * 64, 64), 64), :] = zero
 
     @pl.loop(0, devices // 2)
     def _(pair):
@@ -641,9 +642,10 @@
     out = pl.pallas_call(
         functools.partial(force_kernel, capacity, levels, lines),
         out_shape=jax.ShapeDtypeStruct((levels, lines, tile), jnp.float32),
-        in_specs=[pl.BlockSpec(memory_space=pltpu.VMEM), ANY],
+        in_specs=[ANY, ANY],
         out_specs=ANY,
         scratch_shapes=[
+            pltpu.VMEM(got.shape, jnp.float32),
             pltpu.VMEM((devices * capacity, LANES), jnp.float32),
             pltpu.VMEM((devices // 2, LANES), jnp.int32),
             pltpu.SMEM((devices * capacity,), jnp.int32),
@@ -652,6 +654,7 @@
         ]
         + [pltpu.VMEM((lines * tile + 8, LANES), jnp.float32)] * STREAMS
         + [
+            pltpu.SemaphoreType.DMA,
             pltpu.SemaphoreType.DMA((devices // 2,)),
             pltpu.SemaphoreType.DMA,
             pltpu.SemaphoreType.DMA((lines,)),
@@ -674,7 +677,7 @@
     after_first, got = first_step(adjoint_in, courant, mixing, blocks, lon_count, lat_count)
     forced = add_forcing(got, after_first, capacity)
     swept, sides = second_front(forced, courant, mixing, lon_count, lat_count)
-    return last_sweep(swept, courant, sides, after_first)
+    return last_part(swept, sides, after_first)
 
 
 def solution(mesh):

time: 120 us -> 111 us (0.925)
  Pallas kernels: 119 us -> 111 us
    pallas_call x1, Pallas kernels: 9.38 us -> 5.59 us  [last_part(): pl.pallas_call(last_kernel, out_shape=(jax.ShapeDtypeStruct(cells.shape,...]
    pallas_call x1, Pallas kernels: 55 us -> 52.8 us  [first_step(): pl.pallas_call(functools.partial(first_kernel, lon_count, lat_count), out...]
    pallas_call x1, Pallas kernels: 28.8 us -> 26.6 us  [add_forcing(): pl.pallas_call(functools.partial(force_kernel, capacity, levels, lines),...]
where the time goes in v3:
time: 111 us
  Pallas kernels  111 us (100%)
    pallas_call x1, Pallas kernels, first_step(): pl.pallas_call(functools.partial(first_kernel, lon_count, lat_count), out...  52.8 us
    pallas_call x1, Pallas kernels, add_forcing(): pl.pallas_call(functools.partial(force_kernel, capacity, levels, lines),...  26.6 us
    pallas_call x1, Pallas kernels, second_front(): pl.pallas_call(functools.partial(second_kernel, lon_count, lat_count), ou...  16.6 us
    pallas_call x1, Pallas kernels, pack(): pl.pallas_call(functools.partial(pack_kernel, devices, capacity, levels),...  9.01 us
    pallas_call x1, Pallas kernels, last_part(): pl.pallas_call(last_kernel, out_shape=(jax.ShapeDtypeStruct(cells.shape,...  5.59 us

profile of v3, /device:TPU:1, one launch (start us, length us, event | category | flops | bytes accessed | tf_op | source)
XLA Modules:
  0.0 111.3 jit_solution(64153962398496852)
XLA Ops:
  0.6 9.0 %pack_soundings.1.blocks_hbm = f32[128,40,128]{2,1,0:T(8,128)} custom-call(f32[72,2048]{1,0:T(8,128)} %blocks_ref.1, s32[16,128]{1,0:T(8,128)} %bitcast.6, s32[16,128]{1,0:T(8,128)} %bitcast.7), custom_call_target="tpu_custom_call" | custom-call | tf_op jit(solution)/shard_map/pack_soundings/pallas_call | solution.py:94
  9.6 52.8 %first_step.1 = (f32[2,64,72,128]{3,2,1,0:T(8,128)}, f32[128,40,128]{2,1,0:T(8,128)}) custom-call(f32[72,2,64,128]{3,2,1,0:T(8,128)} %a_hbm.1, f32[2,72,64,128]{3,2,1,0:T(8,128)} %c_hbm.3, f32[71,64,128]{2,1,0:T(8,128)} %m_hbm.3, f32[128,40,128]{2,1,0:T(8,128)} %pack_soundings.1.blocks_hbm), custom_call_target="tpu_custom_call" | custom-call | tf_op jit(solution)/shard_map/first_step/pallas_call | solution.py:453
  62.5 26.6 %add_forcing.1 = f32[72,128,128]{2,1,0:T(8,128)} custom-call(f32[128,40,128]{2,1,0:T(8,128)} %get-tuple-element.6.got_hbm, f32[9216,128]{1,0:T(8,128)} %bitcast.4), custom_call_target="tpu_custom_call" | custom-call | tf_op jit(solution)/shard_map/add_forcing/pallas_call | solution.py:642
  89.1 16.6 %second_front.1 = (f32[72,2,64,128]{3,2,1,0:T(8,128)}, f32[2,2,64,128]{3,2,1,0:T(8,128)}) custom-call(f32[72,2,64,128]{3,2,1,0:T(8,128)} %bitcast.5, f32[2,72,64,128]{3,2,1,0:T(8,128)} %c_hbm.3, f32[71,64,128]{2,1,0:T(8,128)} %m_hbm.3), custom_call_target="tpu_custom_call" | custom-call | tf_op jit(solution)/shard_map/second_front/pallas_call | solution.py:478
  105.7 5.6 %last_part.1 = (f32[72,2,64,128]{3,2,1,0:T(8,128)}, f32[2,64,128]{2,1,0:T(8,128)}) custom-call(f32[72,2,64,128]{3,2,1,0:T(8,128)} %get-tuple-element.8.cells_hbm, f32[2,2,64,128]{3,2,1,0:T(8,128)} %get-tuple-element.9.sides_ref, f32[2,64,72,128]{3,2,1,0:T(8,128)} %get-tuple-element.7.first_hbm), custom_call_target="tpu_custom_call" | custom-call | tf_op jit(solution)/shard_map/last_part/pallas_call | solution.py:536

commit v4 on v3

--- a/solution.py
+++ b/solution.py
@@ -20,92 +20,34 @@
     return lax.broadcasted_iota(jnp.int32, shape, len(shape) - 1)
 
 
-def pack_kernel(
-    devices, capacity, levels, blocks_ref, dest_ref, cell_ref, out_ref, rows, slots, order, order_smem, sems
-):
-    held = blocks_ref.shape[1]
-    chunks = held // LANES
+def slot_table(owner_ref, capacity, held):
     row_id = lax.broadcasted_iota(jnp.int32, (LANES, LANES), 0)
     col_id = lax.broadcasted_iota(jnp.int32, (LANES, LANES), 1)
+    pair_id = lax.broadcasted_iota(jnp.int32, (LANES // 2, LANES), 0)
+    place = lane_iota((LANES // 2, LANES)).astype(jnp.float32)
     before = jnp.where(row_id < col_id, 1.0, 0.0).astype(jnp.bfloat16)
     ones = jnp.ones((LANES, LANES), jnp.bfloat16)
     base = jnp.zeros((LANES, LANES), jnp.float32)
-
-    def to_smem(chunk):
-        return pltpu.make_async_copy(
-            order.at[chunk], order_smem.at[pl.ds(chunk * LANES, LANES)], sems.at[chunk]
-        )
-
-    for chunk in range(chunks):
-        owner = dest_ref[chunk : chunk + 1, :]
-        hot = jnp.broadcast_to(owner, (LANES, LANES)) == row_id
-        hot_f = jnp.where(hot, 1.0, 0.0)
+    table = jnp.zeros((LANES // 2, LANES), jnp.float32)
+    for chunk in range(held // LANES):
+        owner = owner_ref[chunk : chunk + 1, :]
+        hot_f = jnp.where(jnp.broadcast_to(owner, (LANES, LANES)) == row_id, 1.0, 0.0)
         hot_b = hot_f.astype(jnp.bfloat16)
         earlier = jnp.dot(hot_b, before, preferred_element_type=jnp.float32)
-        rank = jnp.sum(hot_f * (earlier + base), axis=0, keepdims=True)
-        order[chunk : chunk + 1, :] = owner * capacity + rank.astype(jnp.int32)
+        rank = jnp.sum(hot_f * (earlier + base), axis=0, keepdims=True).astype(jnp.int32)
         base = base + jnp.dot(hot_b, ones, preferred_element_type=jnp.float32)
-    for chunk in range(chunks):
-        to_smem(chunk).start()
-    blank = jnp.where(lane_iota((64, LANES)) == levels, -1.0, 0.0)
-
-    @pl.loop(0, devices * capacity // 64)
-    def _(i):
-        slots[pl.ds(pl.multiple_of(i * 64, 64), 64), :] = blank
-
-    for chunk in range(chunks):
-        span = slice(chunk * LANES, (chunk + 1) * LANES)
-        tall = jnp.concatenate(
-            [
-                blocks_ref[:, span],
-                jnp.broadcast_to(cell_ref[chunk : chunk + 1, :].astype(jnp.float32), (8, LANES)),
-                jnp.zeros((LANES - levels - 8, LANES), jnp.float32),
-            ],
-            axis=0,
+        pair = lax.shift_right_logical(owner, 1)
+        slot = (owner - 2 * pair) * capacity + rank
+        in_pair = jnp.where(jnp.broadcast_to(pair, pair_id.shape) == pair_id, 1.0, 0.0)
+        in_slot = jnp.where(jnp.broadcast_to(slot, row_id.shape) == row_id, 1.0, 0.0)
+        found = lax.dot_general(
+            jnp.concatenate([in_pair * place, in_pair], axis=0).astype(jnp.bfloat16),
+            in_slot.astype(jnp.bfloat16),
+            (((1,), (1,)), ((), ())),
+            preferred_element_type=jnp.float32,
         )
-        rows[span, :] = tall.T
-    for chunk in range(chunks):
-        to_smem(chunk).wait()
-
-    @pl.loop(0, held // 16)
-    def _(part):
-        for i in range(16):
-            at = part * 16 + i
-            slots[pl.ds(order_smem[at], 1), :] = rows[pl.ds(at, 1), :]
-
-    low = lane_iota((HALF, LANES)) < capacity
-    group = 8
-
-    @pl.loop(0, devices // (2 * group))
-    def _(part):
-        wides = []
-        for i in range(group):
-            at = pl.multiple_of((part * group + i) * LANES, LANES)
-            wides.append(slots[pl.ds(at, LANES), :].T)
-        for i, wide in enumerate(wides):
-            first, second = wide[:HALF], wide[HALF : 2 * HALF]
-            pair = part * group + i
-            out_ref[2 * pair, :HALF] = jnp.where(low, first, pltpu.roll(second, capacity, 1))
-            out_ref[2 * pair + 1, :HALF] = jnp.where(low, pltpu.roll(first, capacity, 1), second)
-
-
-def pack(kernel_blocks, owner, cell, devices, capacity):
-    levels, held = kernel_blocks.shape
-    return pl.pallas_call(
-        functools.partial(pack_kernel, devices, capacity, levels),
-        out_shape=jax.ShapeDtypeStruct((devices, ROOM, LANES), jnp.float32),
-        in_specs=[pl.BlockSpec(memory_space=pltpu.VMEM)] * 3,
-        out_specs=pl.BlockSpec(memory_space=pltpu.VMEM),
-        scratch_shapes=[
-            pltpu.VMEM((held, LANES), jnp.float32),
-            pltpu.VMEM((devices * capacity, LANES), jnp.float32),
-            pltpu.VMEM((held // LANES, LANES), jnp.int32),
-            pltpu.SMEM((held,), jnp.int32),
-            pltpu.SemaphoreType.DMA((held // LANES,)),
-        ],
-        compiler_params=pltpu.CompilerParams(vmem_limit_bytes=VMEM_LIMIT),
-        name="pack_soundings",
-    )(kernel_blocks, owner, cell)
+        table = table + found[: LANES // 2] + found[LANES // 2 :] * (LANES * chunk + 1.0)
+    return table.astype(jnp.int32)
 
 
 def transport_front(lon_count, lat_count, hooks, a_hbm, c_hbm, m_hbm, front):
@@ -336,38 +278,92 @@
             out[k, t, span, :] = cells[k, t, span, :] + jnp.where(ends, turned, 0.0)
 
 
-def peer_at(step, lon_count, lat_count):
-    shift = lax.rem(step * 53, lon_count * lat_count)
+def chip_at(step):
+    shift = lax.rem(step * 27, 64)
     lon, lat = lax.axis_index("lon"), lax.axis_index("lat")
-    wide = lon_count // 8
-    x = lax.rem(lon // 8 + shift // 32, wide)
-    y = lax.rem(lax.rem(lon // 2, 4) + lax.rem(shift // 8, 4), 4)
-    z = lax.rem((lat // 2) * 2 + lax.rem(lon, 2) + lax.rem(shift // 2, 4), 4)
-    core = lax.rem(lat + shift, 2)
-    return x * 8 + y * 2 + lax.rem(z, 2), (z // 2) * 2 + core
-
-
-def first_kernel(lon_count, lat_count, a_hbm, c_hbm, m_hbm, blocks_hbm, out_hbm, got_hbm, *scratch):
-    front, (obuf, store_sem, trade_send, trade_recv, own_sem) = scratch[:FRONT], scratch[FRONT:]
+    x = lax.rem(lon // 8 + shift // 16, 4)
+    y = lax.rem(lax.rem(lon // 2, 4) + lax.rem(shift // 4, 4), 4)
+    z = lax.rem((lat // 2) * 2 + lax.rem(lon, 2) + lax.rem(shift, 4), 4)
+    return x * 8 + y * 2 + lax.rem(z, 2), (z // 2) * 2
+
+
+def first_kernel(
+    lon_count, lat_count, capacity, a_hbm, c_hbm, m_hbm, kernels_hbm, owner_ref, cell_ref, out_hbm, got_hbm, *scratch
+):
+    front, rest = scratch[:FRONT], scratch[FRONT:]
+    (
+        obuf, kernels, rows, table, table_smem, stage, blocks,
+        store_sem, trade_send, trade_recv, own_sem, kernels_sem, table_sem,
+    ) = rest
     c_ref, vbuf, merged = front[1], front[3], front[14]
     levels, tracers, band, tile = vbuf.shape
+    held = kernels.shape[1]
     devices = lon_count * lat_count
-    me = lax.axis_index("lon") * lat_count + lax.axis_index("lat")
+    my_lon, my_lat = lax.axis_index("lon"), lax.axis_index("lat")
+    me = my_lon * lat_count + my_lat
     used = pl.ds(0, HALF)
+    low = lane_iota((HALF, LANES)) < capacity
+
+    def send(lon, lat):
+        pltpu.make_async_remote_copy(
+            src_ref=blocks.at[lon * lat_count + lat, used], dst_ref=got_hbm.at[me, used],
+            send_sem=trade_send, recv_sem=trade_recv,
+            device_id={"lon": lon, "lat": lat}, device_id_type=MESH,
+        ).start()
+
+    def fill(places):
+        wides = []
+        for i, (lon, lat) in enumerate(places):
+            first = ((lon * lat_count + lat) // 2) * LANES
+
+            @pl.loop(0, LANES // 16)
+            def _(part):
+                for j in range(16):
+                    at = part * 16 + j
+                    source = jnp.minimum(jnp.maximum(table_smem[first + at], 0), held + 7)
+                    stage[i, pl.ds(at, 1), :] = rows[pl.ds(source, 1), :]
+
+        for i in range(len(places)):
+            wides.append(stage[i].T)
+        for (lon, lat), wide in zip(places, wides):
+            first, second = wide[:HALF], wide[HALF : 2 * HALF]
+            at = lon * lat_count + lat
+            blocks[at, :HALF] = jnp.where(low, first, pltpu.roll(second, capacity, 1))
+            blocks[at + 1, :HALF] = jnp.where(low, pltpu.roll(first, capacity, 1), second)
 
     def trade(begin, end):
         @pl.loop(begin, end)
-        def _(i):
-            lon, lat = peer_at(i, lon_count, lat_count)
-            pltpu.make_async_remote_copy(
-                src_ref=blocks_hbm.at[lon * lat_count + lat, used], dst_ref=got_hbm.at[me, used],
-                send_sem=trade_send, recv_sem=trade_recv,
-                device_id={"lon": lon, "lat": lat}, device_id_type=MESH,
-            ).start()
-
-    early = 1 + devices // 5
+        def _(part):
+            places = [chip_at(part * 4 + i) for i in range(4)]
+            fill(places)
+            for lon, lat in places:
+                send(lon, lat)
+                send(lon, lat + 1)
+
+    own = pltpu.make_async_copy(blocks.at[me, used], got_hbm.at[me, used], own_sem)
+
+    def trade_first():
+        @pl.loop(0, devices // 2)
+        def _(pair):
+            to_smem(pair).wait()
+
+        places = [chip_at(i) for i in range(4)]
+        fill(places)
+        send(my_lon, my_lat + 1 - 2 * lax.rem(my_lat, 2))
+        own.start()
+        for lon, lat in places[1:]:
+            send(lon, lat)
+            send(lon, lat + 1)
+        trade(1, 4)
+
+    def to_smem(pair):
+        return pltpu.make_async_copy(
+            table.at[pair], table_smem.at[pl.ds(pair * LANES, LANES)], table_sem.at[pair]
+        )
 
     def at_entry():
+        load = pltpu.make_async_copy(kernels_hbm, kernels, kernels_sem)
+        load.start()
         barrier = pltpu.get_barrier_semaphore()
 
         @pl.loop(1, devices)
@@ -378,7 +374,24 @@
                 device_id_type=MESH,
             )
 
-        pltpu.make_async_copy(blocks_hbm.at[me], got_hbm.at[me], own_sem).start()
+        table[...] = slot_table(owner_ref, capacity, held) + 7
+
+        @pl.loop(0, devices // 2)
+        def _(pair):
+            to_smem(pair).start()
+
+        load.wait()
+        rows[0:8, :] = jnp.where(lane_iota((8, LANES)) == levels, -1.0, 0.0)
+        for chunk in range(held // LANES):
+            tall = jnp.concatenate(
+                [
+                    kernels[:, chunk * LANES : (chunk + 1) * LANES],
+                    jnp.broadcast_to(cell_ref[chunk : chunk + 1, :].astype(jnp.float32), (8, LANES)),
+                    jnp.zeros((LANES - levels - 8, LANES), jnp.float32),
+                ],
+                axis=0,
+            )
+            rows[8 + chunk * LANES : 8 + (chunk + 1) * LANES, :] = tall.T
 
     def before_rows():
         pl.semaphore_wait(pltpu.get_barrier_semaphore(), devices - 1)
@@ -386,7 +399,7 @@
     def main_sweep():
         sweep_all(c_ref, vbuf, obuf, lambda g: None)
 
-    hooks = (at_entry, before_rows, lambda: trade(1, early), lambda: trade(early, devices), main_sweep)
+    hooks = (at_entry, before_rows, trade_first, lambda: trade(4, devices // 8), main_sweep)
     transport_front(lon_count, lat_count, hooks, a_hbm, c_hbm, m_hbm, front)
 
     def stored(t, r):
@@ -399,12 +412,12 @@
             for r in range(8):
                 stored(t, g * 8 + r).start()
 
-    pltpu.make_async_copy(blocks_hbm.at[me], got_hbm.at[me], own_sem).wait()
+    own.wait()
     most = pl.ds(0, devices - 1)
     pltpu.make_async_remote_copy(
-        src_ref=blocks_hbm.at[most, used], dst_ref=got_hbm.at[most, used],
+        src_ref=blocks.at[most, used], dst_ref=got_hbm.at[most, used],
         send_sem=trade_send, recv_sem=trade_recv,
-        device_id={"lon": lax.axis_index("lon"), "lat": lax.rem(lax.axis_index("lat") + 1, lat_count)},
+        device_id={"lon": my_lon, "lat": lax.rem(my_lat + 1, lat_count)},
         device_id_type=MESH,
     ).wait()
 
@@ -448,29 +461,41 @@
         stored(g).wait()
 
 
-def first_step(state, courant, mixing, blocks, lon_count, lat_count):
+def first_step(state, courant, mixing, kernel_blocks, owner, cell, lon_count, lat_count, capacity):
     levels, tracers, band, tile = state.shape
+    devices = lon_count * lat_count
+    held = kernel_blocks.shape[1]
+    f32 = jnp.float32
+    small = pl.BlockSpec(memory_space=pltpu.VMEM)
     return pl.pallas_call(
-        functools.partial(first_kernel, lon_count, lat_count),
+        functools.partial(first_kernel, lon_count, lat_count, capacity),
         out_shape=(
-            jax.ShapeDtypeStruct((tracers, band, levels, tile), jnp.float32),
-            jax.ShapeDtypeStruct(blocks.shape, jnp.float32),
+            jax.ShapeDtypeStruct((tracers, band, levels, tile), f32),
+            jax.ShapeDtypeStruct((devices, ROOM, LANES), f32),
         ),
-        in_specs=[ANY] * 4,
+        in_specs=[ANY] * 4 + [small] * 2,
         out_specs=(ANY, ANY),
         scratch_shapes=front_scratch(levels, tracers, band, tile)
         + [
-            pltpu.VMEM((levels, tracers, band, tile), jnp.float32),
+            pltpu.VMEM((levels, tracers, band, tile), f32),
+            pltpu.VMEM((levels, held), f32),
+            pltpu.VMEM((held + 8, LANES), f32),
+            pltpu.VMEM((devices // 2, LANES), jnp.int32),
+            pltpu.SMEM((devices * capacity,), jnp.int32),
+            pltpu.VMEM((4, LANES, LANES), f32),
+            pltpu.VMEM((devices, ROOM, LANES), f32),
             pltpu.SemaphoreType.DMA((tracers * band,)),
             pltpu.SemaphoreType.DMA,
             pltpu.SemaphoreType.DMA,
             pltpu.SemaphoreType.DMA,
+            pltpu.SemaphoreType.DMA,
+            pltpu.SemaphoreType.DMA((devices // 2,)),
         ],
         compiler_params=pltpu.CompilerParams(
             collective_id=0, has_side_effects=True, vmem_limit_bytes=VMEM_LIMIT
         ),
         name="first_step",
-    )(state, courant, mixing, blocks)
+    )(state, courant, mixing, kernel_blocks, owner, cell)
 
 
 def second_front(state, courant, mixing, lon_count, lat_count):
@@ -589,10 +614,8 @@
             ids[pl.ds(pair, 1), :] = jnp.where(cell < 0, cells_all, cell)
             wide = jnp.concatenate([first, second, jnp.zeros((LANES - 2 * HALF, LANES), jnp.float32)], axis=0)
             rows[pl.ds(pl.multiple_of(pair * LANES, LANES), LANES), :] = wide.T
-
-    @pl.loop(0, devices // 2)
-    def _(pair):
-        to_smem(pair).start()
+        for i in range(group):
+            to_smem(part * group + i).start()
 
     @pl.loop(0, devices // 2)
     def _(pair):
@@ -673,8 +696,9 @@
     capacity = 4 * held // devices
     owner = sounding_dest.reshape(held // LANES, LANES)
     cell = sounding_cell.reshape(held // LANES, LANES)
-    blocks = pack(kernel_blocks, owner, cell, devices, capacity)
-    after_first, got = first_step(adjoint_in, courant, mixing, blocks, lon_count, lat_count)
+    after_first, got = first_step(
+        adjoint_in, courant, mixing, kernel_blocks, owner, cell, lon_count, lat_count, capacity
+    )
     forced = add_forcing(got, after_first, capacity)
     swept, sides = second_front(forced, courant, mixing, lon_count, lat_count)
     return last_part(swept, sides, after_first)

time: 111 us -> 103 us (0.928)
  Pallas kernels: 111 us -> 102 us
    pallas_call x2 -> x1, Pallas kernels: 61.8 us -> 55.2 us  [first_step(): pl.pallas_call(functools.partial(first_kernel, lon_count, lat_count, capa...]
    pallas_call x1, Pallas kernels: 16.6 us -> 15.1 us  [second_front(): pl.pallas_call(functools.partial(second_kernel, lon_count, lat_count), ou...]
where the time goes in v4:
time: 103 us
  Pallas kernels  102 us (99%)
    pallas_call x1, Pallas kernels, first_step(): pl.pallas_call(functools.partial(first_kernel, lon_count, lat_count, capa...  55.2 us
    pallas_call x1, Pallas kernels, add_forcing(): pl.pallas_call(functools.partial(force_kernel, capacity, levels, lines),...  26.3 us
    pallas_call x1, Pallas kernels, second_front(): pl.pallas_call(functools.partial(second_kernel, lon_count, lat_count), ou...  15.1 us
    pallas_call x1, Pallas kernels, last_part(): pl.pallas_call(last_kernel, out_shape=(jax.ShapeDtypeStruct(cells.shape,...  5.59 us

profile of v4, /device:TPU:1, one launch (start us, length us, event | category | flops | bytes accessed | tf_op | source)
XLA Modules:
  0.0 102.9 jit_solution(4029384026317216464)
XLA Ops:
  0.6 55.2 %first_step.1 = (f32[2,64,72,128]{3,2,1,0:T(8,128)}, f32[128,40,128]{2,1,0:T(8,128)}) custom-call(f32[72,2,64,128]{3,2,1,0:T(8,128)} %a_hbm.1, f32[2,72,64,128]{3,2,1,0:T(8,128)} %c_hbm.3, f32[71,64,128]{2,1,0:T(8,128)} %m_hbm.3, f32[72,2048]{1,0:T(8,128)} %kernels_hbm.1, s32[16,128]{1,0:T(8,128)} %bitcast.6, s32[16,128]{1,0:T(8,128)} %bitcast.7), custom_call_target="tpu_custom_call" | custom-call | tf_op jit(solution)/shard_map/first_step/pallas_call | solution.py:470
  55.8 26.3 %add_forcing.1 = f32[72,128,128]{2,1,0:T(8,128)} custom-call(f32[128,40,128]{2,1,0:T(8,128)} %get-tuple-element.6.got_hbm, f32[9216,128]{1,0:T(8,128)} %bitcast.4), custom_call_target="tpu_custom_call" | custom-call | tf_op jit(solution)/shard_map/add_forcing/pallas_call | solution.py:665
  82.2 15.1 %second_front.1 = (f32[72,2,64,128]{3,2,1,0:T(8,128)}, f32[2,2,64,128]{3,2,1,0:T(8,128)}) custom-call(f32[72,2,64,128]{3,2,1,0:T(8,128)} %bitcast.5, f32[2,72,64,128]{3,2,1,0:T(8,128)} %c_hbm.3, f32[71,64,128]{2,1,0:T(8,128)} %m_hbm.3), custom_call_target="tpu_custom_call" | custom-call | tf_op jit(solution)/shard_map/second_front/pallas_call | solution.py:503
  97.3 5.6 %last_part.1 = (f32[72,2,64,128]{3,2,1,0:T(8,128)}, f32[2,64,128]{2,1,0:T(8,128)}) custom-call(f32[72,2,64,128]{3,2,1,0:T(8,128)} %get-tuple-element.8.cells_hbm, f32[2,2,64,128]{3,2,1,0:T(8,128)} %get-tuple-element.9.sides_ref, f32[2,64,72,128]{3,2,1,0:T(8,128)} %get-tuple-element.7.first_hbm), custom_call_target="tpu_custom_call" | custom-call | tf_op jit(solution)/shard_map/last_part/pallas_call | solution.py:561

commit v5 on v4

--- a/solution.py
+++ b/solution.py
@@ -316,11 +316,11 @@
         for i, (lon, lat) in enumerate(places):
             first = ((lon * lat_count + lat) // 2) * LANES
 
-            @pl.loop(0, LANES // 16)
+            @pl.loop(0, LANES // 64)
             def _(part):
-                for j in range(16):
-                    at = part * 16 + j
-                    source = jnp.minimum(jnp.maximum(table_smem[first + at], 0), held + 7)
+                for j in range(64):
+                    at = part * 64 + j
+                    source = table_smem[first + at] & (2 * held - 1)
                     stage[i, pl.ds(at, 1), :] = rows[pl.ds(source, 1), :]
 
         for i in range(len(places)):
@@ -374,7 +374,7 @@
                 device_id_type=MESH,
             )
 
-        table[...] = slot_table(owner_ref, capacity, held) + 7
+        table[...] = jnp.clip(slot_table(owner_ref, capacity, held) + 7, 0, held + 7)
 
         @pl.loop(0, devices // 2)
         def _(pair):
@@ -479,7 +479,7 @@
         + [
             pltpu.VMEM((levels, tracers, band, tile), f32),
             pltpu.VMEM((levels, held), f32),
-            pltpu.VMEM((held + 8, LANES), f32),
+            pltpu.VMEM((2 * held, LANES), f32),
             pltpu.VMEM((devices // 2, LANES), jnp.int32),
             pltpu.SMEM((devices * capacity,), jnp.int32),
             pltpu.VMEM((4, LANES, LANES), f32),
@@ -637,6 +637,8 @@
 
     def stored(line):
         return pltpu.make_async_copy(total.at[level_rows(line)], out_hbm.at[:, line, :], store_sem.at[line])
+
+    group = 16
 
     @pl.loop(0, lines // group)
     def _(part):

time: 103 us -> 100 us (0.971)
  Pallas kernels: 102 us -> 99 us
    pallas_call x1, Pallas kernels: 55.2 us -> 52.8 us  [first_step(): pl.pallas_call(functools.partial(first_kernel, lon_count, lat_count, capa...]
where the time goes in v5:
time: 100 us; the launch traced here: 99.7 us
  Pallas kernels  99 us (99%)
    pallas_call x1, Pallas kernels, first_step(): pl.pallas_call(functools.partial(first_kernel, lon_count, lat_count, capa...  52.8 us
    pallas_call x1, Pallas kernels, add_forcing(): pl.pallas_call(functools.partial(force_kernel, capacity, levels, lines),...  25.9 us
    pallas_call x1, Pallas kernels, second_front(): pl.pallas_call(functools.partial(second_kernel, lon_count, lat_count), ou...  14.9 us
    pallas_call x1, Pallas kernels, last_part(): pl.pallas_call(last_kernel, out_shape=(jax.ShapeDtypeStruct(cells.shape,...  5.59 us

profile of v5, /device:TPU:1, one launch (start us, length us, event | category | flops | bytes accessed | tf_op | source)
XLA Modules:
  0.0 99.7 jit_solution(12451541465284119248)
XLA Ops:
  0.6 52.8 %first_step.1 = (f32[2,64,72,128]{3,2,1,0:T(8,128)}, f32[128,40,128]{2,1,0:T(8,128)}) custom-call(f32[72,2,64,128]{3,2,1,0:T(8,128)} %a_hbm.1, f32[2,72,64,128]{3,2,1,0:T(8,128)} %c_hbm.3, f32[71,64,128]{2,1,0:T(8,128)} %m_hbm.3, f32[72,2048]{1,0:T(8,128)} %kernels_hbm.1, s32[16,128]{1,0:T(8,128)} %bitcast.6, s32[16,128]{1,0:T(8,128)} %bitcast.7), custom_call_target="tpu_custom_call" | custom-call | tf_op jit(solution)/shard_map/first_step/pallas_call | solution.py:470
  53.4 25.9 %add_forcing.1 = f32[72,128,128]{2,1,0:T(8,128)} custom-call(f32[128,40,128]{2,1,0:T(8,128)} %get-tuple-element.6.got_hbm, f32[9216,128]{1,0:T(8,128)} %bitcast.4), custom_call_target="tpu_custom_call" | custom-call | tf_op jit(solution)/shard_map/add_forcing/pallas_call | solution.py:667
  79.3 14.9 %second_front.1 = (f32[72,2,64,128]{3,2,1,0:T(8,128)}, f32[2,2,64,128]{3,2,1,0:T(8,128)}) custom-call(f32[72,2,64,128]{3,2,1,0:T(8,128)} %bitcast.5, f32[2,72,64,128]{3,2,1,0:T(8,128)} %c_hbm.3, f32[71,64,128]{2,1,0:T(8,128)} %m_hbm.3), custom_call_target="tpu_custom_call" | custom-call | tf_op jit(solution)/shard_map/second_front/pallas_call | solution.py:503
  94.1 5.6 %last_part.1 = (f32[72,2,64,128]{3,2,1,0:T(8,128)}, f32[2,64,128]{2,1,0:T(8,128)}) custom-call(f32[72,2,64,128]{3,2,1,0:T(8,128)} %get-tuple-element.8.cells_hbm, f32[2,2,64,128]{3,2,1,0:T(8,128)} %get-tuple-element.9.sides_ref, f32[2,64,72,128]{3,2,1,0:T(8,128)} %get-tuple-element.7.first_hbm), custom_call_target="tpu_custom_call" | custom-call | tf_op jit(solution)/shard_map/last_part/pallas_call | solution.py:561

commit v6 on v5

--- a/solution.py
+++ b/solution.py
@@ -392,14 +392,14 @@
                 axis=0,
             )
             rows[8 + chunk * LANES : 8 + (chunk + 1) * LANES, :] = tall.T
-
-    def before_rows():
-        pl.semaphore_wait(pltpu.get_barrier_semaphore(), devices - 1)
+        pl.semaphore_wait(barrier, devices - 1)
+        trade_first()
 
     def main_sweep():
         sweep_all(c_ref, vbuf, obuf, lambda g: None)
 
-    hooks = (at_entry, before_rows, trade_first, lambda: trade(4, devices // 8), main_sweep)
+    groups = devices // 8
+    hooks = (at_entry, lambda: None, lambda: trade(4, 9), lambda: trade(9, groups), main_sweep)
     transport_front(lon_count, lat_count, hooks, a_hbm, c_hbm, m_hbm, front)
 
     def stored(t, r):

time: 100 us -> 105 us (1.050)
  Pallas kernels: 99 us -> 104 us
    pallas_call x1, Pallas kernels: 52.8 us -> 58 us  [first_step(): pl.pallas_call(functools.partial(first_kernel, lon_count, lat_count, capa...]
where the time goes in v6:
time: 105 us
  Pallas kernels  104 us (99%)
    pallas_call x1, Pallas kernels, first_step(): pl.pallas_call(functools.partial(first_kernel, lon_count, lat_count, capa...  58 us
    pallas_call x1, Pallas kernels, add_forcing(): pl.pallas_call(functools.partial(force_kernel, capacity, levels, lines),...  25.8 us
    pallas_call x1, Pallas kernels, second_front(): pl.pallas_call(functools.partial(second_kernel, lon_count, lat_count), ou...  14.9 us
    pallas_call x1, Pallas kernels, last_part(): pl.pallas_call(last_kernel, out_shape=(jax.ShapeDtypeStruct(cells.shape,...  5.59 us

profile of v6, /device:TPU:1, one launch (start us, length us, event | category | flops | bytes accessed | tf_op | source)
XLA Modules:
  0.0 104.9 jit_solution(4102352404840128405)
XLA Ops:
  0.6 58.0 %first_step.1 = (f32[2,64,72,128]{3,2,1,0:T(8,128)}, f32[128,40,128]{2,1,0:T(8,128)}) custom-call(f32[72,2,64,128]{3,2,1,0:T(8,128)} %a_hbm.1, f32[2,72,64,128]{3,2,1,0:T(8,128)} %c_hbm.3, f32[71,64,128]{2,1,0:T(8,128)} %m_hbm.3, f32[72,2048]{1,0:T(8,128)} %kernels_hbm.1, s32[16,128]{1,0:T(8,128)} %bitcast.6, s32[16,128]{1,0:T(8,128)} %bitcast.7), custom_call_target="tpu_custom_call" | custom-call | tf_op jit(solution)/shard_map/first_step/pallas_call | solution.py:470
  58.6 25.8 %add_forcing.1 = f32[72,128,128]{2,1,0:T(8,128)} custom-call(f32[128,40,128]{2,1,0:T(8,128)} %get-tuple-element.6.got_hbm, f32[9216,128]{1,0:T(8,128)} %bitcast.4), custom_call_target="tpu_custom_call" | custom-call | tf_op jit(solution)/shard_map/add_forcing/pallas_call | solution.py:667
  84.5 14.9 %second_front.1 = (f32[72,2,64,128]{3,2,1,0:T(8,128)}, f32[2,2,64,128]{3,2,1,0:T(8,128)}) custom-call(f32[72,2,64,128]{3,2,1,0:T(8,128)} %bitcast.5, f32[2,72,64,128]{3,2,1,0:T(8,128)} %c_hbm.3, f32[71,64,128]{2,1,0:T(8,128)} %m_hbm.3), custom_call_target="tpu_custom_call" | custom-call | tf_op jit(solution)/shard_map/second_front/pallas_call | solution.py:503
  99.3 5.6 %last_part.1 = (f32[72,2,64,128]{3,2,1,0:T(8,128)}, f32[2,64,128]{2,1,0:T(8,128)}) custom-call(f32[72,2,64,128]{3,2,1,0:T(8,128)} %get-tuple-element.8.cells_hbm, f32[2,2,64,128]{3,2,1,0:T(8,128)} %get-tuple-element.9.sides_ref, f32[2,64,72,128]{3,2,1,0:T(8,128)} %get-tuple-element.7.first_hbm), custom_call_target="tpu_custom_call" | custom-call | tf_op jit(solution)/shard_map/last_part/pallas_call | solution.py:561
